TPU v7x, 256 devices: a whole 4x4x8 slice. The times are simulated.
256 devices in a mesh: row: 8 (over x, core), col: 32 (over z, y).
Axes of the slice: x: 4, y: 4, z: 8, core: 2. Of those that a mesh axis runs over, the one named last changes fastest.
Arguments:
- panel: bfloat16 [65536, 512], P('row', 'col'), may hold values from -0.0234375 to 0.0234375
- pheno: bfloat16 [65536, 8192], P('row', 'col'), may hold values from -48 to 48
- kin_values: float32 [512], replicated, may hold values from 0.1 to 10
- trait_values: float32 [128], replicated, may hold values from 0.1 to 10
- trait_basis: float32 [128, 128], replicated, may hold values from -0.5 to 0.5
Outputs:
- coeffs: float32 [512, 8192], P('row', 'col')
- genetic: bfloat16 [65536, 8192], P('row', 'col')
All inputs are finite; a program needn't handle non-finite values.
Results may differ from a plain program's by a relative error of at most 0.0049.
Values may be sent and summed in bfloat16 or wider, within the bound.
No kernel may reach another device: no remote copies, remote signals or barrier semaphores. Data moves between devices by JAX's collectives and lax.ppermute only.
A program may use at most 64 MiB of HBM per device.

v0:
```python
import jax
import jax.numpy as jnp
from jax import lax
from jax.sharding import PartitionSpec as P

TRAITS = 128
SETS_DEV = 2


def cut_along(shard, dim, count):
    before, after = (shard.shape[:dim], shard.shape[dim + 1 :])
    return jnp.moveaxis(shard.reshape(*before, count, -1, *after), dim, 0)


def sum_at_owner(shard, axis, dim):
    count = lax.axis_size(axis)
    pieces = lax.all_to_all(cut_along(shard, dim, count), axis, 0, 0, tiled=True)
    return jnp.sum(pieces, axis=0)


def laid_out(pieces, dim):
    dims = list(pieces.shape[1:])
    dims[dim] *= pieces.shape[0]
    return jnp.moveaxis(pieces, 0, dim).reshape(dims)


def copy_for_each(shard, axis):
    count = lax.axis_size(axis)
    return lax.all_to_all(
        jnp.broadcast_to(shard[None], (count, *shard.shape)), axis, 0, 0, tiled=True
    )


def gather_directly(shard, axis, dim):
    return laid_out(copy_for_each(shard, axis), dim)


def local(panel, pheno, kin_values, trait_values, trait_basis):
    col_count = lax.axis_size("col")
    columns = pheno.shape[1]
    traits_here = TRAITS // col_count
    set_count = SETS_DEV * col_count
    whole_panel = lax.all_gather(panel, "col", axis=1, tiled=True)
    partial_value = lax.dot_general(
        whole_panel, pheno, (((0,), (0,)), ((), ())), preferred_element_type=jnp.float32
    )
    summed = sum_at_owner(partial_value, "row", 0)
    first_row = lax.axis_index("row") * summed.shape[0]
    share_rows = summed.shape[0]
    by_trait = summed.reshape(share_rows, traits_here, set_count).transpose(0, 2, 1)
    by_trait = by_trait.reshape(share_rows, set_count * traits_here)
    grouped = lax.all_to_all(by_trait, "col", split_axis=1, concat_axis=1, tiled=True)
    grouped = grouped.reshape(share_rows, col_count, SETS_DEV, traits_here).transpose(0, 2, 1, 3)
    grouped = grouped.reshape(share_rows, SETS_DEV, TRAITS)
    rotated = jnp.einsum("rst,tj->rsj", grouped, trait_basis, precision=lax.Precision.HIGHEST)
    kin_rows = lax.dynamic_slice_in_dim(kin_values, first_row, share_rows, 0)
    product = kin_rows[:, None] * trait_values[None, :]
    scaled = rotated * (product / (product + 1.0))[:, None, :]
    unrotated = jnp.einsum("rsj,tj->rst", scaled, trait_basis, precision=lax.Precision.HIGHEST)
    outgoing = unrotated.reshape(share_rows, SETS_DEV, col_count, traits_here).transpose(0, 2, 1, 3)
    outgoing = outgoing.reshape(share_rows, col_count * SETS_DEV * traits_here)
    returned = lax.all_to_all(outgoing, "col", split_axis=1, concat_axis=1, tiled=True)
    coeffs = returned.reshape(share_rows, set_count, traits_here).transpose(0, 2, 1)
    coeffs = coeffs.reshape(share_rows, columns)
    coeffs_low = gather_directly(coeffs.astype(jnp.bfloat16), "row", 0)
    genetic = jnp.dot(whole_panel, coeffs_low, preferred_element_type=jnp.float32)
    return (coeffs, genetic.astype(jnp.bfloat16))


def solution(mesh):
    return jax.shard_map(
        local,
        mesh=mesh,
        in_specs=(P("row", "col"), P("row", "col"), P(), P(), P()),
        out_specs=(P("row", "col"), P("row", "col")),
        check_vma=False,
    )
```

profile of v0, /device:TPU:1, one launch (start us, length us, event | category | flops | bytes accessed | tf_op | source)
XLA Modules:
  0.0 199.2 jit_solution(6438156583780600088)
XLA Ops:
  7.2 0.0 copy-start
  7.2 0.0 all-gather.2.cloned.1.call-start
  7.2 0.7 all-gather.2.cloned.1.call-update
  7.9 0.0 copy-start.2
  7.9 104.7 %all-gather.2.cloned.1.call-done = bf16[8192,512]{0,1:T(8,128)(2,1)} async-done(((bf16[8192,16]{0,1:T(8,128)(2,1)}), bf16[8192,512]{0,1:T(8,128)(2,1)}) %all-gather.2.cloned.1.call-update) | async-done | bytes 8388624 | tf_op jit(solution)/shard_map/all_gather | solution.py:43
  112.6 7.7 %fusion.4 = f32[512,256]{1,0:T(8,128)} fusion(bf16[8192,512]{0,1:T(8,128)(2,1)} %all-gather.2.cloned.1.call-done, bf16[8192,256]{1,0:T(8,128)(2,1)} %param.6), kind=kOutput, calls=%fused_computation.9 | convolution fusion | flops 2147483648 | bytes 13107200 | tf_op jit(solution)/shard_map/dot_general | solution.py:44
  120.3 5.3 %all-to-all-start = ((f32[8,64,256]{2,1,0:T(8,128)}), f32[8,64,256]{2,1,0:T(8,128)S(1)}, u32[]{:S(2)}, u32[]{:S(2)}) async-start(f32[8,64,256]{2,1,0:T(8,128)} %bitcast), calls=%async_computation | async-start | bytes 1048576 | tf_op jit(solution)/shard_map/all_to_all | solution.py:17
  125.6 0.8 dynamic_slice.3
  126.4 8.7 %all-to-all-done = f32[8,64,256]{2,1,0:T(8,128)S(1)} async-done(((f32[8,64,256]{2,1,0:T(8,128)}), f32[8,64,256]{2,1,0:T(8,128)S(1)}, u32[]{:S(2)}, u32[]{:S(2)}) %all-to-all-start) | async-done | bytes 524320 | tf_op jit(solution)/shard_map/all_to_all | solution.py:17
  135.1 0.1 reshape.69
  135.2 0.1 copy.23
  135.4 0.8 reshape.77
  136.1 5.3 %all-to-all-start.1 = ((f32[32,1,512]{2,1,0:T(1,128)}), f32[32,1,512]{2,1,0:T(1,128)S(1)}, u32[]{:S(2)}, u32[]{:S(2)}) async-start(f32[32,1,512]{2,1,0:T(1,128)} %reshape.77), calls=%async_computation.1 | async-start | bytes 131072 | tf_op jit(solution)/shard_map/all_to_all | solution.py:52
  141.5 0.1 add_divide_fusion
  141.6 8.7 %all-to-all-done.1 = f32[32,1,512]{2,1,0:T(1,128)S(1)} async-done(((f32[32,1,512]{2,1,0:T(1,128)}), f32[32,1,512]{2,1,0:T(1,128)S(1)}, u32[]{:S(2)}, u32[]{:S(2)}) %all-to-all-start.1) | async-done | bytes 65568 | tf_op jit(solution)/shard_map/all_to_all | solution.py:52
  150.3 0.5 broadcast.18
  150.8 0.8 reduce
  151.7 0.1 reshape.78
  151.8 0.1 copy.25
  151.9 0.4 convolution_multiply_fusion
  152.3 0.3 fusion.1
  152.6 0.1 copy.35
  152.7 0.1 reshape.79
  152.8 12.0 %all_to_all.28 = f32[32,1,512]{2,1,0:T(1,128)S(1)} all-to-all(f32[32,1,512]{2,1,0:T(1,128)S(1)} %reshape.79), channel_id=1, replica_groups=mesh['row'=8,'col'=32] {'col'}, dimensions={0} | all-to-all | bytes 131072 | tf_op jit(solution)/shard_map/all_to_all | solution.py:62
  164.8 0.8 reduce.1
  165.6 0.1 reshape.80
  165.7 0.1 copy.30
  165.8 0.1 reshape.74
  166.0 12.3 %all_to_all.29 = bf16[8,64,256]{2,1,0:T(8,128)(2,1)S(1)} all-to-all(bf16[8,64,256]{2,1,0:T(8,128)(2,1)S(1)} %broadcast_in_dim.2), channel_id=1, replica_groups=mesh['row'=8,'col'=32] {'row'}, dimensions={0} | all-to-all | bytes 524288 | tf_op jit(solution)/shard_map/all_to_all | solution.py:29
  178.3 7.7 %fusion = bf16[8192,256]{0,1:T(8,128)(2,1)} fusion(bf16[512,256]{1,0:T(8,128)(2,1)S(1)} %bitcast.37, bf16[8192,512]{0,1:T(8,128)(2,1)} %all-gather.2.cloned.1.call-done), kind=kOutput, calls=%fused_computation.1 | convolution fusion | flops 2149580800 | bytes 12845056 | tf_op jit(solution)/shard_map/dot_general | solution.py:66
  186.0 6.4 %copy.31 = bf16[8192,256]{1,0:T(8,128)(2,1)} copy(bf16[8192,256]{0,1:T(8,128)(2,1)} %fusion) | data formatting | bytes 8388608
  192.4 0.0 copy-done.1
  (9 shorter events, 0.1 us)
Async XLA Ops:
  7.2 144.7 %copy-start = (f32[128,128]{1,0:T(8,128)S(1)}, f32[128,128]{1,0:T(8,128)}, u32[]{:S(2)}) copy-start(f32[128,128]{1,0:T(8,128)} %param.9) | copy-start | bytes 196612
  7.2 105.4 %all-gather.2.cloned.1.call-start = ((), (), s32[]{:S(2)}) async-start(), calls=%async_computation.4 | async-start | bytes 8650752 | tf_op jit(solution)/shard_map/all_gather | solution.py:43
  7.9 133.6 %copy-start.2 = (f32[128]{0:T(128)S(1)}, f32[128]{0:T(128)}, u32[]{:S(2)}) copy-start(f32[128]{0:T(128)} %param.8) | copy-start | bytes 1540
  120.3 14.8 %all-to-all-start = ((f32[8,64,256]{2,1,0:T(8,128)}), f32[8,64,256]{2,1,0:T(8,128)S(1)}, u32[]{:S(2)}, u32[]{:S(2)}) async-start(f32[8,64,256]{2,1,0:T(8,128)} %bitcast), calls=%async_computation | async-start | bytes 1048576 | tf_op jit(solution)/shard_map/all_to_all | solution.py:17
  136.1 14.2 %all-to-all-start.1 = ((f32[32,1,512]{2,1,0:T(1,128)}), f32[32,1,512]{2,1,0:T(1,128)S(1)}, u32[]{:S(2)}, u32[]{:S(2)}) async-start(f32[32,1,512]{2,1,0:T(1,128)} %reshape.77), calls=%async_computation.1 | async-start | bytes 131072 | tf_op jit(solution)/shard_map/all_to_all | solution.py:52
  166.0 26.4 %copy-start.1 = (f32[64,256]{1,0:T(8,128)}, f32[64,256]{1,0:T(8,128)S(1)}, u32[]{:S(2)}) copy-start(f32[64,256]{1,0:T(8,128)S(1)} %reshape.74) | copy-start | bytes 196612
Sparse Core Ops, SparseCore 0:
  10.6 101.9 all-gather.1
where the time goes:
time: 200 us; the launch traced here: 199 us
  waiting for transfers between devices  123 us (62%)
  blocking collectives  24.2 us (12%)
  matrix products  16.1 us (8%)
  between operations  14.2 us (7%)
  starting transfers between devices  10.7 us (5%)
  local copies, waits for them, and re-layouts  9.41 us (5%)
    all_gather x1, waiting for transfers between devices, local(): whole_panel = lax.all_gather(panel, 'col', axis=1, tiled=True)  105 us
    all_to_all x1, blocking collectives, copy_for_each(): lax.all_to_all(jnp.broadcast_to(shard[None], (count, *shard.shape)), axis...  12.3 us
    all_to_all x1, blocking collectives, local(): lax.all_to_all(outgoing, 'col', split_axis=1, concat_axis=1, tiled=True)  12 us
    all_to_all x1, waiting for transfers between devices, local(): lax.all_to_all(by_trait, 'col', split_axis=1, concat_axis=1, tiled=True)  8.74 us
    all_to_all x1, waiting for transfers between devices, sum_at_owner(): lax.all_to_all(cut_along(shard, dim, count), axis, 0, 0, tiled=True)  8.73 us
    dot_general x1, matrix products, local(): jnp.dot(whole_panel, coeffs_low, preferred_element_type=jnp.float32)  7.71 us
    dot_general x1, matrix products, local(): lax.dot_general(whole_panel, pheno, (((0,), (0,)), ((), ())), preferred_e...  7.7 us
    unnamed x12, local copies, waits for them, and re-layouts  7.44 us
  transfers between devices with their start and end apart: 3, of which 3 were waited for; matrix products, arithmetic and copies ran while one was open for 0% of the time, Pallas kernels for 0%

commit v1 on v0

v1 whole, which is shorter than its diff:
```python
import jax
import jax.numpy as jnp
from jax import lax
from jax.sharding import Mesh, PartitionSpec as P

ROW = ("x", "core")
COL = ("z", "y")
ALL = ROW + COL
NX, NC, NZ, NY = 4, 2, 8, 4
SHARE = 16
TRAITS = 128
SETS = 64
LA = 3328


def shift(value, axis, count, step):
    return lax.ppermute(value, axis, [(i, (i + step) % count) for i in range(count)])


def ring(own, axis, count):
    before, after = {0: own}, {0: own}
    for k in range(1, count // 2):
        before[-k] = shift(before[1 - k], axis, count, 1)
        after[k] = shift(after[k - 1], axis, count, -1)
    half = own.shape[1] // 256 * 128
    far = jnp.concatenate(
        [
            shift(before[1 - count // 2][:, :half], axis, count, 1),
            shift(after[count // 2 - 1][:, half:], axis, count, -1),
        ],
        axis=1,
    )
    return {k % count: v for k, v in {**before, **after, count // 2: far}.items()}


def gather_panel(own):
    a, b = {}, {}
    by_y = ring(own, "y", NY)
    for dy, block in by_y.items():
        b[dy, 0] = block[:, LA:]
    along = ring(jnp.concatenate([by_y[dy][:, :LA] for dy in range(NY)], 0), "z", NZ)
    for dz, block in along.items():
        for dy in range(NY):
            a[dy, dz] = block[dy * SHARE : (dy + 1) * SHARE]
    by_z = ring(own[:, LA:], "z", NZ)
    for near in ((7, 1, 6, 2), (5, 3, 4)):
        group = ring(jnp.concatenate([by_z[dz] for dz in near], 0), "y", NY)
        for dy, block in group.items():
            for n, dz in enumerate(near):
                b[dy, dz] = block[n * SHARE : (n + 1) * SHARE]
    order = [(dy, dz) for dy in range(NY) for dz in range(NZ)]
    return jnp.concatenate(
        [jnp.concatenate([a[k], b[k]], 1) for k in order], 0
    )


def turn(value, axis, by):
    count = value.shape[axis]
    twice = jnp.concatenate([value, value], axis)
    return lax.dynamic_slice_in_dim(twice, count - by, count, axis)


def local(panel, pheno, kin_values, trait_values, trait_basis):
    z, y = lax.axis_index("z"), lax.axis_index("y")
    row = lax.axis_index("x") * NC + lax.axis_index("core")
    whole = gather_panel(panel.T)
    part = jnp.dot(whole, pheno, preferred_element_type=jnp.float32)
    part = part.reshape(NY, NZ, SHARE, TRAITS // 32 * SETS)
    part = turn(turn(part, 1, z), 0, y).reshape(NY, 128, 4, SETS)
    outgoing = part.astype(jnp.bfloat16).transpose(3, 0, 2, 1).reshape(256, 4, 128)
    incoming = lax.all_to_all(outgoing, ALL, 0, 0, tiled=True)
    summed = jnp.sum(incoming.reshape(8, TRAITS, 128).astype(jnp.float32), 0)
    kin = lax.dynamic_index_in_dim(kin_values.reshape(NZ, NY, SHARE), y, 1, False)
    gain = trait_values[:, None] * kin.reshape(1, 128)
    high = lax.Precision.HIGHEST
    rotated = jnp.einsum("tj,tp->jp", trait_basis, summed, precision=high)
    scaled = rotated * (gain / (gain + 1.0))
    unrotated = jnp.einsum("tj,jp->tp", trait_basis, scaled, precision=high)
    low = unrotated.astype(jnp.bfloat16).reshape(1, 32, 4, 128)
    back = jnp.broadcast_to(low, (8, 32, 4, 128)).reshape(256, 4, 128)
    back = lax.all_to_all(back, ALL, 0, 0, tiled=True)
    coeffs_low = back.reshape(SETS, NY, 4, 128).transpose(1, 3, 2, 0)
    coeffs_low = coeffs_low.reshape(NY, NZ, SHARE, 256)
    coeffs = lax.dynamic_index_in_dim(coeffs_low, row, 1, False)
    coeffs = coeffs.reshape(NY * SHARE, 256).astype(jnp.float32)
    here = turn(turn(coeffs_low, 1, (NZ - z) % NZ), 0, (NY - y) % NY).reshape(512, 256)
    genetic = lax.dot_general(
        whole, here, (((0,), (0,)), ((), ())), preferred_element_type=jnp.float32
    )
    return coeffs, genetic.astype(jnp.bfloat16)


def solution(mesh):
    split = Mesh(mesh.devices.reshape(NX, NC, NZ, NY), ALL)
    return jax.shard_map(
        local,
        mesh=split,
        in_specs=(P(ROW, COL), P(ROW, COL), P(), P(), P()),
        out_specs=(P(ROW, COL), P(ROW, COL)),
        check_vma=False,
    )
```

time: 200 us -> 161 us (0.81)
  starting transfers between devices: 10.7 us -> 62.6 us
  waiting for transfers between devices: 123 us -> 74.9 us
  blocking collectives: 24.2 us -> 0 us
  between operations: 14.2 us -> 1.41 us
  matrix products: 16.1 us -> 10.7 us
    all_gather x1 -> x0, waiting for transfers between devices: 105 us -> none  [local(): whole_panel = lax.all_gather(panel, 'col', axis=1, tiled=True)]
    ppermute x0 -> x28, waiting for transfers between devices: none -> 45.5 us  [shift(): lax.ppermute(value, axis, [(i, (i + step) % count) for i in range(count)])]
    ppermute x0 -> x28, starting transfers between devices: none -> 32.4 us  [shift(): lax.ppermute(value, axis, [(i, (i + step) % count) for i in range(count)])]
    all_to_all x2 -> x0, blocking collectives: 24.2 us -> none  [the longest x1 12.3 us: copy_for_each(): lax.all_to_all(jnp.broadcast_to(shard[None], (count, *shard.shape)), axis...]
    all_to_all x2, starting transfers between devices: 10.7 us -> 30.2 us  [the longest x1 23.9 us: local(): incoming = lax.all_to_all(outgoing, ALL, 0, 0, tiled=True)]
    all_to_all x2, waiting for transfers between devices: 17.5 us -> 29.4 us  [the longest x1 14.8 us: local(): back = lax.all_to_all(back, ALL, 0, 0, tiled=True)]
    dot_general x4, matrix products: 16.1 us -> 10.7 us  [the longest x1 7.81 us: local(): lax.dot_general(whole, here, (((0,), (0,)), ((), ())), preferred_element_...]
    unnamed x12 -> x21, local copies, waits for them, and re-layouts: 7.44 us -> 2.61 us
  transfers between devices with their start and end apart: 3 -> 30, of which waited for: 3 -> 15; matrix products, arithmetic and copies ran while one was open for 0% -> 3% of each run, Pallas kernels for 0% -> 0%
where the time goes in v1:
time: 161 us; the launch traced here: 160 us
  waiting for transfers between devices  74.9 us (47%)
  starting transfers between devices  62.6 us (39%)
  matrix products  10.7 us (7%)
  local copies, waits for them, and re-layouts  8.36 us (5%)
  other arithmetic  2.48 us (2%)
    ppermute x28, waiting for transfers between devices, shift(): lax.ppermute(value, axis, [(i, (i + step) % count) for i in range(count)])  45.5 us
    ppermute x28, starting transfers between devices, shift(): lax.ppermute(value, axis, [(i, (i + step) % count) for i in range(count)])  32.4 us
    all_to_all x1, starting transfers between devices, local(): incoming = lax.all_to_all(outgoing, ALL, 0, 0, tiled=True)  23.9 us
    all_to_all x1, waiting for transfers between devices, local(): back = lax.all_to_all(back, ALL, 0, 0, tiled=True)  14.8 us
    all_to_all x1, waiting for transfers between devices, local(): incoming = lax.all_to_all(outgoing, ALL, 0, 0, tiled=True)  14.5 us
    dot_general x1, matrix products, local(): lax.dot_general(whole, here, (((0,), (0,)), ((), ())), preferred_element_...  7.81 us
    all_to_all x1, starting transfers between devices, local(): back = lax.all_to_all(back, ALL, 0, 0, tiled=True)  6.23 us
  transfers between devices with their start and end apart: 30, of which 15 were waited for; matrix products, arithmetic and copies ran while one was open for 3% of the time, Pallas kernels for 0%

profile of v1, /device:TPU:1, one launch (start us, length us, event | category | flops | bytes accessed | tf_op | source)
XLA Modules:
  0.0 160.4 jit_solution(5320154018006008020)
XLA Ops:
  0.6 2.2 %collective-permute-start.1 = (bf16[16,8192]{1,0:T(8,128)(2,1)}, bf16[16,8192]{1,0:T(8,128)(2,1)S(1)}, u32[]{:S(2)}, u32[]{:S(2)}) collective-permute-start(bf16[16,8192]{1,0:T(8,128)(2,1)} %bitcast.38), channel_id=1, source_target_pairs={{0,1},{1,2},{2,3},{3,0},{4,5},{5,6},{6,7},{7,4},{8,9},{9,10},{10,1... | collective-permute-start | bytes 786440 | tf_op jit(solution)/shard_map/ppermute | solution.py:17
  2.8 1.5 collective-permute-start
  5.3 5.7 %collective-permute-start.4 = (bf16[16,4864]{1,0:T(8,128)(2,1)S(1)}, bf16[16,4864]{1,0:T(8,128)(2,1)S(1)}, u32[]{:S(2)}, u32[]{:S(2)}) collective-permute-start(bf16[16,4864]{1,0:T(8,128)(2,1)S(1)} %slice.272), channel_id=1, source_target_pairs={{0,28},{4,0},{8,4},{12,8},{16,12},{20,16},{24,20},{28,24},{1,29},{... | collective-permute-start | bytes 466952 | tf_op jit(solution)/shard_map/ppermute | solution.py:17
  11.0 1.7 %constant_dynamic-update-slice_fusion.12 = bf16[512,8192]{1,0:T(8,128)(2,1)} fusion(bf16[8192,16]{0,1:T(8,128)(2,1)} %param.5), kind=kLoop, calls=%fused_computation.66 | loop fusion | bytes 524288
  13.6 2.7 %collective-permute-done.14 = bf16[16,4864]{1,0:T(8,128)(2,1)S(1)} collective-permute-done((bf16[16,4864]{1,0:T(8,128)(2,1)S(1)}, bf16[16,4864]{1,0:T(8,128)(2,1)S(1)}, u32[]{:S(2)}, u32[]{:S(2)}) %collective-permute-start.14) | collective-permute-done | bytes 155680 | tf_op jit(solution)/shard_map/ppermute | solution.py:17
  16.3 2.7 %collective-permute-start.6 = (bf16[16,4864]{1,0:T(8,128)(2,1)S(1)}, bf16[16,4864]{1,0:T(8,128)(2,1)S(1)}, u32[]{:S(2)}, u32[]{:S(2)}) collective-permute-start(bf16[16,4864]{1,0:T(8,128)(2,1)S(1)} %collective-permute-done.4), channel_id=1, source_target_pairs={{0,28},{4,0},{8,4},{12,8},{16,12},{20,16},{24,20},{28,24},{1,29},{... | collective-permute-start | bytes 466952 | tf_op jit(solution)/shard_map/ppermute | solution.py:17
  19.2 2.7 %collective-permute-start.21 = (bf16[16,4096]{1,0:T(8,128)(2,1)S(1)}, bf16[16,4096]{1,0:T(8,128)(2,1)S(1)}, u32[]{:S(2)}, u32[]{:S(2)}) collective-permute-start(bf16[16,4096]{1,0:T(8,128)(2,1)S(1)} %slice.297), channel_id=1, source_target_pairs={{0,3},{1,0},{2,1},{3,2},{4,7},{5,4},{6,5},{7,6},{8,11},{9,8},{10,9... | collective-permute-start | bytes 393224 | tf_op jit(solution)/shard_map/ppermute | solution.py:17
  22.0 2.4 %collective-permute-start.8 = (bf16[16,4864]{1,0:T(8,128)(2,1)S(1)}, bf16[16,4864]{1,0:T(8,128)(2,1)S(1)}, u32[]{:S(2)}, u32[]{:S(2)}) collective-permute-start(bf16[16,4864]{1,0:T(8,128)(2,1)S(1)} %collective-permute-done.6), channel_id=1, source_target_pairs={{0,28},{4,0},{8,4},{12,8},{16,12},{20,16},{24,20},{28,24},{1,29},{... | collective-permute-start | bytes 466952 | tf_op jit(solution)/shard_map/ppermute | solution.py:17
  24.4 1.5 collective-permute-start.19
  26.0 3.7 %collective-permute-done.16 = bf16[16,4864]{1,0:T(8,128)(2,1)S(1)} collective-permute-done((bf16[16,4864]{1,0:T(8,128)(2,1)S(1)}, bf16[16,4864]{1,0:T(8,128)(2,1)S(1)}, u32[]{:S(2)}, u32[]{:S(2)}) %collective-permute-start.16) | collective-permute-done | bytes 155680 | tf_op jit(solution)/shard_map/ppermute | solution.py:17
  29.7 2.7 %collective-permute-start.18 = (bf16[16,2432]{1,0:T(8,128)(2,1)S(1)}, bf16[16,2432]{1,0:T(8,128)(2,1)S(1)}, u32[]{:S(2)}, u32[]{:S(2)}) collective-permute-start(bf16[16,2432]{1,0:T(8,128)(2,1)S(1)} %slice.279), channel_id=1, source_target_pairs={{0,28},{4,0},{8,4},{12,8},{16,12},{20,16},{24,20},{28,24},{1,29},{... | collective-permute-start | bytes 233480 | tf_op jit(solution)/shard_map/ppermute | solution.py:17
  32.5 2.7 %collective-permute-done.17 = bf16[16,2432]{1,0:T(8,128)(2,1)S(1)} collective-permute-done((bf16[16,2432]{1,0:T(8,128)(2,1)S(1)}, bf16[16,2432]{1,0:T(8,128)(2,1)S(1)}, u32[]{:S(2)}, u32[]{:S(2)}) %collective-permute-start.17) | collective-permute-done | bytes 77856 | tf_op jit(solution)/shard_map/ppermute | solution.py:17
  35.2 1.5 collective-permute-start.9
  36.7 6.4 %collective-permute-done.3 = bf16[64,3328]{1,0:T(8,128)(2,1)S(1)} collective-permute-done((bf16[64,3328]{1,0:T(8,128)(2,1)S(1)}, bf16[64,3328]{1,0:T(8,128)(2,1)S(1)}, u32[]{:S(2)}, u32[]{:S(2)}) %collective-permute-start.3) | collective-permute-done | bytes 426016 | tf_op jit(solution)/shard_map/ppermute | solution.py:17
  43.1 1.6 collective-permute-start.20
  47.3 3.5 %collective-permute-done.20 = bf16[48,4864]{1,0:T(8,128)(2,1)S(1)} collective-permute-done((bf16[48,4864]{1,0:T(8,128)(2,1)S(1)}, bf16[48,4864]{1,0:T(8,128)(2,1)S(1)}, u32[]{:S(2)}, u32[]{:S(2)}) %collective-permute-start.20) | collective-permute-done | bytes 466976 | tf_op jit(solution)/shard_map/ppermute | solution.py:17
  50.9 2.6 %collective-permute-done.25 = bf16[48,4864]{1,0:T(8,128)(2,1)S(1)} collective-permute-done((bf16[48,4864]{1,0:T(8,128)(2,1)S(1)}, bf16[48,4864]{1,0:T(8,128)(2,1)S(1)}, u32[]{:S(2)}, u32[]{:S(2)}) %collective-permute-start.25) | collective-permute-done | bytes 466976 | tf_op jit(solution)/shard_map/ppermute | solution.py:17
  53.7 5.1 %collective-permute-done.23 = bf16[64,2432]{1,0:T(8,128)(2,1)S(1)} collective-permute-done((bf16[64,2432]{1,0:T(8,128)(2,1)S(1)}, bf16[64,2432]{1,0:T(8,128)(2,1)S(1)}, u32[]{:S(2)}, u32[]{:S(2)}) %collective-permute-start.23) | collective-permute-done | bytes 311328 | tf_op jit(solution)/shard_map/ppermute | solution.py:17
  58.9 3.9 %collective-permute-done.24 = bf16[64,2432]{1,0:T(8,128)(2,1)S(1)} collective-permute-done((bf16[64,2432]{1,0:T(8,128)(2,1)S(1)}, bf16[64,2432]{1,0:T(8,128)(2,1)S(1)}, u32[]{:S(2)}, u32[]{:S(2)}) %collective-permute-start.24) | collective-permute-done | bytes 311328 | tf_op jit(solution)/shard_map/ppermute | solution.py:17
  62.8 1.4 collective-permute-start.27
  64.2 1.3 collective-permute-done.26
  65.6 3.0 %collective-permute-done.27 = bf16[48,2432]{1,0:T(8,128)(2,1)S(1)} collective-permute-done((bf16[48,2432]{1,0:T(8,128)(2,1)S(1)}, bf16[48,2432]{1,0:T(8,128)(2,1)S(1)}, u32[]{:S(2)}, u32[]{:S(2)}) %collective-permute-start.27) | collective-permute-done | bytes 233504 | tf_op jit(solution)/shard_map/ppermute | solution.py:17
  68.8 1.4 collective-permute-start.11
  70.3 7.0 %collective-permute-done.11 = bf16[64,3328]{1,0:T(8,128)(2,1)S(1)} collective-permute-done((bf16[64,3328]{1,0:T(8,128)(2,1)S(1)}, bf16[64,3328]{1,0:T(8,128)(2,1)S(1)}, u32[]{:S(2)}, u32[]{:S(2)}) %collective-permute-start.11) | collective-permute-done | bytes 426016 | tf_op jit(solution)/shard_map/ppermute | solution.py:17
  77.6 2.8 %collective-permute-start.13 = (bf16[64,1664]{1,0:T(8,128)(2,1)S(1)}, bf16[64,1664]{1,0:T(8,128)(2,1)S(1)}, u32[]{:S(2)}, u32[]{:S(2)}) collective-permute-start(bf16[64,1664]{1,0:T(8,128)(2,1)S(1)} %slice.276), channel_id=1, source_target_pairs={{0,28},{4,0},{8,4},{12,8},{16,12},{20,16},{24,20},{28,24},{1,29},{... | collective-permute-start | bytes 638984 | tf_op jit(solution)/shard_map/ppermute | solution.py:17
  80.6 2.8 %collective-permute-done.12 = bf16[64,1664]{1,0:T(8,128)(2,1)S(1)} collective-permute-done((bf16[64,1664]{1,0:T(8,128)(2,1)S(1)}, bf16[64,1664]{1,0:T(8,128)(2,1)S(1)}, u32[]{:S(2)}, u32[]{:S(2)}) %collective-permute-start.12) | collective-permute-done | bytes 213024 | tf_op jit(solution)/shard_map/ppermute | solution.py:17
  84.9 2.3 %fusion.23 = bf16[512,256]{1,0:T(8,128)(2,1)S(1)} fusion(bf16[512,8192]{1,0:T(8,128)(2,1)S(1)} %maximum_dynamic-update-slice_fusion, bf16[8192,256]{1,0:T(8,128)(2,1)S(1)} %copy-done.4), kind=kOutput, calls=%fused_computation.83 | convolution fusion | flops 2147483648 | bytes 12845056 | tf_op jit(solution)/shard_map/dot_general | solution.py:67
  89.8 23.9 %all-to-all-start = ((bf16[256,4,128]{2,1,0:T(4,128)(2,1)}), bf16[256,4,128]{2,1,0:T(4,128)(2,1)S(1)}, u32[]{:S(2)}, u32[]{:S(2)}) async-start(bf16[256,4,128]{2,1,0:T(4,128)(2,1)} %copy.13), calls=%async_computation | async-start | bytes 524288 | tf_op jit(solution)/shard_map/all_to_all | solution.py:71
  113.9 14.5 %all-to-all-done = bf16[256,4,128]{2,1,0:T(4,128)(2,1)S(1)} async-done(((bf16[256,4,128]{2,1,0:T(4,128)(2,1)}), bf16[256,4,128]{2,1,0:T(4,128)(2,1)S(1)}, u32[]{:S(2)}, u32[]{:S(2)}) %all-to-all-start) | async-done | bytes 262176 | tf_op jit(solution)/shard_map/all_to_all | solution.py:71
  129.8 6.2 %all-to-all-start.1 = ((bf16[256,4,128]{2,1,0:T(4,128)(2,1)}), bf16[256,4,128]{2,1,0:T(4,128)(2,1)S(1)}, u32[]{:S(2)}, u32[]{:S(2)}) async-start(bf16[256,4,128]{2,1,0:T(4,128)(2,1)} %bitcast.8), calls=%async_computation.1 | async-start | bytes 524288 | tf_op jit(solution)/shard_map/all_to_all | solution.py:81
  136.1 14.8 %all-to-all-done.1 = bf16[256,4,128]{2,1,0:T(4,128)(2,1)S(1)} async-done(((bf16[256,4,128]{2,1,0:T(4,128)(2,1)}), bf16[256,4,128]{2,1,0:T(4,128)(2,1)S(1)}, u32[]{:S(2)}, u32[]{:S(2)}) %all-to-all-start.1) | async-done | bytes 262176 | tf_op jit(solution)/shard_map/all_to_all | solution.py:81
  151.9 7.8 %convolution_convert_fusion = bf16[8192,256]{1,0:T(8,128)(2,1)} fusion(bf16[512,8192]{1,0:T(8,128)(2,1)} %copy-done.2, bf16[512,256]{1,0:T(8,128)(2,1)S(1)} %bitcast.42), kind=kOutput, calls=%fused_computation | convolution fusion | flops 2149580800 | bytes 12845056 | tf_op jit(solution)/shard_map/dot_general | solution.py:87
  (133 shorter events, 12.7 us)
Async XLA Ops:
  0.6 127.8 %copy-start = (f32[128,128]{1,0:T(8,128)S(1)}, f32[128,128]{1,0:T(8,128)}, u32[]{:S(2)}) copy-start(f32[128,128]{1,0:T(8,128)} %param.9) | copy-start | bytes 196612
  0.6 18.4 %collective-permute-start.1 = (bf16[16,8192]{1,0:T(8,128)(2,1)}, bf16[16,8192]{1,0:T(8,128)(2,1)S(1)}, u32[]{:S(2)}, u32[]{:S(2)}) collective-permute-start(bf16[16,8192]{1,0:T(8,128)(2,1)} %bitcast.38), channel_id=1, source_target_pairs={{0,1},{1,2},{2,3},{3,0},{4,5},{5,6},{6,7},{7,4},{8,9},{9,10},{10,1... | collective-permute-start | bytes 786440 | tf_op jit(solution)/shard_map/ppermute | solution.py:17
  2.8 16.3 %collective-permute-start = (bf16[16,8192]{1,0:T(8,128)(2,1)}, bf16[16,8192]{1,0:T(8,128)(2,1)S(1)}, u32[]{:S(2)}, u32[]{:S(2)}) collective-permute-start(bf16[16,8192]{1,0:T(8,128)(2,1)} %bitcast.39), channel_id=1, source_target_pairs={{0,3},{1,0},{2,1},{3,2},{4,7},{5,4},{6,5},{7,6},{8,11},{9,8},{10,9... | collective-permute-start | bytes 786440 | tf_op jit(solution)/shard_map/ppermute | solution.py:17
  5.3 11.0 %collective-permute-start.4 = (bf16[16,4864]{1,0:T(8,128)(2,1)S(1)}, bf16[16,4864]{1,0:T(8,128)(2,1)S(1)}, u32[]{:S(2)}, u32[]{:S(2)}) collective-permute-start(bf16[16,4864]{1,0:T(8,128)(2,1)S(1)} %slice.272), channel_id=1, source_target_pairs={{0,28},{4,0},{8,4},{12,8},{16,12},{20,16},{24,20},{28,24},{1,29},{... | collective-permute-start | bytes 466952 | tf_op jit(solution)/shard_map/ppermute | solution.py:17
  11.0 5.3 %collective-permute-start.14 = (bf16[16,4864]{1,0:T(8,128)(2,1)S(1)}, bf16[16,4864]{1,0:T(8,128)(2,1)S(1)}, u32[]{:S(2)}, u32[]{:S(2)}) collective-permute-start(bf16[16,4864]{1,0:T(8,128)(2,1)S(1)} %slice.272), channel_id=1, source_target_pairs={{0,4},{4,8},{8,12},{12,16},{16,20},{20,24},{24,28},{28,0},{1,5},{5... | collective-permute-start | bytes 466952 | tf_op jit(solution)/shard_map/ppermute | solution.py:17
  16.3 8.1 %collective-permute-start.15 = (bf16[16,4864]{1,0:T(8,128)(2,1)S(1)}, bf16[16,4864]{1,0:T(8,128)(2,1)S(1)}, u32[]{:S(2)}, u32[]{:S(2)}) collective-permute-start(bf16[16,4864]{1,0:T(8,128)(2,1)S(1)} %collective-permute-done.14), channel_id=1, source_target_pairs={{0,4},{4,8},{8,12},{12,16},{16,20},{20,24},{24,28},{28,0},{1,5},{5... | collective-permute-start | bytes 466952 | tf_op jit(solution)/shard_map/ppermute | solution.py:17
  16.3 5.7 %collective-permute-start.6 = (bf16[16,4864]{1,0:T(8,128)(2,1)S(1)}, bf16[16,4864]{1,0:T(8,128)(2,1)S(1)}, u32[]{:S(2)}, u32[]{:S(2)}) collective-permute-start(bf16[16,4864]{1,0:T(8,128)(2,1)S(1)} %collective-permute-done.4), channel_id=1, source_target_pairs={{0,28},{4,0},{8,4},{12,8},{16,12},{20,16},{24,20},{28,24},{1,29},{... | collective-permute-start | bytes 466952 | tf_op jit(solution)/shard_map/ppermute | solution.py:17
  19.1 6.7 %collective-permute-start.2 = (bf16[16,4096]{1,0:T(8,128)(2,1)S(1)}, bf16[16,4096]{1,0:T(8,128)(2,1)S(1)}, u32[]{:S(2)}, u32[]{:S(2)}) collective-permute-start(bf16[16,4096]{1,0:T(8,128)(2,1)S(1)} %slice.268), channel_id=1, source_target_pairs={{0,1},{1,2},{2,3},{3,0},{4,5},{5,6},{6,7},{7,4},{8,9},{9,10},{10,1... | collective-permute-start | bytes 393224 | tf_op jit(solution)/shard_map/ppermute | solution.py:17
  19.2 65.2 %collective-permute-start.21 = (bf16[16,4096]{1,0:T(8,128)(2,1)S(1)}, bf16[16,4096]{1,0:T(8,128)(2,1)S(1)}, u32[]{:S(2)}, u32[]{:S(2)}) collective-permute-start(bf16[16,4096]{1,0:T(8,128)(2,1)S(1)} %slice.297), channel_id=1, source_target_pairs={{0,3},{1,0},{2,1},{3,2},{4,7},{5,4},{6,5},{7,6},{8,11},{9,8},{10,9... | collective-permute-start | bytes 393224 | tf_op jit(solution)/shard_map/ppermute | solution.py:17
  22.0 7.7 %collective-permute-start.8 = (bf16[16,4864]{1,0:T(8,128)(2,1)S(1)}, bf16[16,4864]{1,0:T(8,128)(2,1)S(1)}, u32[]{:S(2)}, u32[]{:S(2)}) collective-permute-start(bf16[16,4864]{1,0:T(8,128)(2,1)S(1)} %collective-permute-done.6), channel_id=1, source_target_pairs={{0,28},{4,0},{8,4},{12,8},{16,12},{20,16},{24,20},{28,24},{1,29},{... | collective-permute-start | bytes 466952 | tf_op jit(solution)/shard_map/ppermute | solution.py:17
  24.4 5.3 %collective-permute-start.16 = (bf16[16,4864]{1,0:T(8,128)(2,1)S(1)}, bf16[16,4864]{1,0:T(8,128)(2,1)S(1)}, u32[]{:S(2)}, u32[]{:S(2)}) collective-permute-start(bf16[16,4864]{1,0:T(8,128)(2,1)S(1)} %collective-permute-done.15), channel_id=1, source_target_pairs={{0,4},{4,8},{8,12},{12,16},{16,20},{20,24},{24,28},{28,0},{1,5},{5... | collective-permute-start | bytes 466952 | tf_op jit(solution)/shard_map/ppermute | solution.py:17
  24.4 21.2 %collective-permute-start.19 = (bf16[64,4864]{1,0:T(8,128)(2,1)S(1)}, bf16[64,4864]{1,0:T(8,128)(2,1)S(1)}, u32[]{:S(2)}, u32[]{:S(2)}) collective-permute-start(bf16[64,4864]{1,0:T(8,128)(2,1)S(1)} %constant_dynamic-update-slice_fusion.2), channel_id=1, source_target_pairs={{0,3},{1,0},{2,1},{3,2},{4,7},{5,4},{6,5},{7,6},{8,11},{9,8},{10,9... | collective-permute-start | bytes 1867784 | tf_op jit(solution)/shard_map/ppermute | solution.py:17
  25.9 20.9 %collective-permute-start.22 = (bf16[64,4864]{1,0:T(8,128)(2,1)S(1)}, bf16[64,4864]{1,0:T(8,128)(2,1)S(1)}, u32[]{:S(2)}, u32[]{:S(2)}) collective-permute-start(bf16[64,4864]{1,0:T(8,128)(2,1)S(1)} %constant_dynamic-update-slice_fusion.2), channel_id=1, source_target_pairs={{0,1},{1,2},{2,3},{3,0},{4,5},{5,6},{6,7},{7,4},{8,9},{9,10},{10,1... | collective-permute-start | bytes 1867784 | tf_op jit(solution)/shard_map/ppermute | solution.py:17
  29.7 5.5 %collective-permute-start.17 = (bf16[16,2432]{1,0:T(8,128)(2,1)S(1)}, bf16[16,2432]{1,0:T(8,128)(2,1)S(1)}, u32[]{:S(2)}, u32[]{:S(2)}) collective-permute-start(bf16[16,2432]{1,0:T(8,128)(2,1)S(1)} %slice.278), channel_id=1, source_target_pairs={{0,4},{4,8},{8,12},{12,16},{16,20},{20,24},{24,28},{28,0},{1,5},{5... | collective-permute-start | bytes 233480 | tf_op jit(solution)/shard_map/ppermute | solution.py:17
  29.7 5.5 %collective-permute-start.18 = (bf16[16,2432]{1,0:T(8,128)(2,1)S(1)}, bf16[16,2432]{1,0:T(8,128)(2,1)S(1)}, u32[]{:S(2)}, u32[]{:S(2)}) collective-permute-start(bf16[16,2432]{1,0:T(8,128)(2,1)S(1)} %slice.279), channel_id=1, source_target_pairs={{0,28},{4,0},{8,4},{12,8},{16,12},{20,16},{24,20},{28,24},{1,29},{... | collective-permute-start | bytes 233480 | tf_op jit(solution)/shard_map/ppermute | solution.py:17
  35.2 7.9 %collective-permute-start.3 = (bf16[64,3328]{1,0:T(8,128)(2,1)S(1)}, bf16[64,3328]{1,0:T(8,128)(2,1)S(1)}, u32[]{:S(2)}, u32[]{:S(2)}) collective-permute-start(bf16[64,3328]{1,0:T(8,128)(2,1)S(1)} %pad_maximum_fusion), channel_id=1, source_target_pairs={{0,28},{4,0},{8,4},{12,8},{16,12},{20,16},{24,20},{28,24},{1,29},{... | collective-permute-start | bytes 1277960 | tf_op jit(solution)/shard_map/ppermute | solution.py:17
  35.2 9.5 %collective-permute-start.9 = (bf16[64,3328]{1,0:T(8,128)(2,1)S(1)}, bf16[64,3328]{1,0:T(8,128)(2,1)S(1)}, u32[]{:S(2)}, u32[]{:S(2)}) collective-permute-start(bf16[64,3328]{1,0:T(8,128)(2,1)S(1)} %pad_maximum_fusion), channel_id=1, source_target_pairs={{0,4},{4,8},{8,12},{12,16},{16,20},{20,24},{24,28},{28,0},{1,5},{5... | collective-permute-start | bytes 1277960 | tf_op jit(solution)/shard_map/ppermute | solution.py:17
  43.1 7.7 %collective-permute-start.20 = (bf16[48,4864]{1,0:T(8,128)(2,1)S(1)}, bf16[48,4864]{1,0:T(8,128)(2,1)S(1)}, u32[]{:S(2)}, u32[]{:S(2)}) collective-permute-start(bf16[48,4864]{1,0:T(8,128)(2,1)S(1)} %maximum_maximum_fusion), channel_id=1, source_target_pairs={{0,3},{1,0},{2,1},{3,2},{4,7},{5,4},{6,5},{7,6},{8,11},{9,8},{10,9... | collective-permute-start | bytes 1400840 | tf_op jit(solution)/shard_map/ppermute | solution.py:17
  44.7 8.7 %collective-permute-start.25 = (bf16[48,4864]{1,0:T(8,128)(2,1)S(1)}, bf16[48,4864]{1,0:T(8,128)(2,1)S(1)}, u32[]{:S(2)}, u32[]{:S(2)}) collective-permute-start(bf16[48,4864]{1,0:T(8,128)(2,1)S(1)} %maximum_maximum_fusion), channel_id=1, source_target_pairs={{0,1},{1,2},{2,3},{3,0},{4,5},{5,6},{6,7},{7,4},{8,9},{9,10},{10,1... | collective-permute-start | bytes 1400840 | tf_op jit(solution)/shard_map/ppermute | solution.py:17
  45.6 23.1 %collective-permute-start.5 = (bf16[64,3328]{1,0:T(8,128)(2,1)S(1)}, bf16[64,3328]{1,0:T(8,128)(2,1)S(1)}, u32[]{:S(2)}, u32[]{:S(2)}) collective-permute-start(bf16[64,3328]{1,0:T(8,128)(2,1)S(1)} %collective-permute-done.3), channel_id=1, source_target_pairs={{0,28},{4,0},{8,4},{12,8},{16,12},{20,16},{24,20},{28,24},{1,29},{... | collective-permute-start | bytes 1277960 | tf_op jit(solution)/shard_map/ppermute | solution.py:17
  46.8 22.0 %collective-permute-start.10 = (bf16[64,3328]{1,0:T(8,128)(2,1)S(1)}, bf16[64,3328]{1,0:T(8,128)(2,1)S(1)}, u32[]{:S(2)}, u32[]{:S(2)}) collective-permute-start(bf16[64,3328]{1,0:T(8,128)(2,1)S(1)} %collective-permute-done.9), channel_id=1, source_target_pairs={{0,4},{4,8},{8,12},{12,16},{16,20},{20,24},{24,28},{28,0},{1,5},{5... | collective-permute-start | bytes 1277960 | tf_op jit(solution)/shard_map/ppermute | solution.py:17
  50.8 8.0 %collective-permute-start.23 = (bf16[64,2432]{1,0:T(8,128)(2,1)S(1)}, bf16[64,2432]{1,0:T(8,128)(2,1)S(1)}, u32[]{:S(2)}, u32[]{:S(2)}) collective-permute-start(bf16[64,2432]{1,0:T(8,128)(2,1)S(1)} %slice.299), channel_id=1, source_target_pairs={{0,1},{1,2},{2,3},{3,0},{4,5},{5,6},{6,7},{7,4},{8,9},{9,10},{10,1... | collective-permute-start | bytes 933896 | tf_op jit(solution)/shard_map/ppermute | solution.py:17
  53.4 9.3 %collective-permute-start.24 = (bf16[64,2432]{1,0:T(8,128)(2,1)S(1)}, bf16[64,2432]{1,0:T(8,128)(2,1)S(1)}, u32[]{:S(2)}, u32[]{:S(2)}) collective-permute-start(bf16[64,2432]{1,0:T(8,128)(2,1)S(1)} %slice.300), channel_id=1, source_target_pairs={{0,3},{1,0},{2,1},{3,2},{4,7},{5,4},{6,5},{7,6},{8,11},{9,8},{10,9... | collective-permute-start | bytes 933896 | tf_op jit(solution)/shard_map/ppermute | solution.py:17
  58.8 6.7 %collective-permute-start.26 = (bf16[48,2432]{1,0:T(8,128)(2,1)S(1)}, bf16[48,2432]{1,0:T(8,128)(2,1)S(1)}, u32[]{:S(2)}, u32[]{:S(2)}) collective-permute-start(bf16[48,2432]{1,0:T(8,128)(2,1)S(1)} %slice.305), channel_id=1, source_target_pairs={{0,1},{1,2},{2,3},{3,0},{4,5},{5,6},{6,7},{7,4},{8,9},{9,10},{10,1... | collective-permute-start | bytes 700424 | tf_op jit(solution)/shard_map/ppermute | solution.py:17
  62.8 5.8 %collective-permute-start.27 = (bf16[48,2432]{1,0:T(8,128)(2,1)S(1)}, bf16[48,2432]{1,0:T(8,128)(2,1)S(1)}, u32[]{:S(2)}, u32[]{:S(2)}) collective-permute-start(bf16[48,2432]{1,0:T(8,128)(2,1)S(1)} %slice.306), channel_id=1, source_target_pairs={{0,3},{1,0},{2,1},{3,2},{4,7},{5,4},{6,5},{7,6},{8,11},{9,8},{10,9... | collective-permute-start | bytes 700424 | tf_op jit(solution)/shard_map/ppermute | solution.py:17
  68.7 8.9 %collective-permute-start.7 = (bf16[64,3328]{1,0:T(8,128)(2,1)S(1)}, bf16[64,3328]{1,0:T(8,128)(2,1)S(1)}, u32[]{:S(2)}, u32[]{:S(2)}) collective-permute-start(bf16[64,3328]{1,0:T(8,128)(2,1)S(1)} %collective-permute-done.5), channel_id=1, source_target_pairs={{0,28},{4,0},{8,4},{12,8},{16,12},{20,16},{24,20},{28,24},{1,29},{... | collective-permute-start | bytes 1277960 | tf_op jit(solution)/shard_map/ppermute | solution.py:17
  68.8 8.6 %collective-permute-start.11 = (bf16[64,3328]{1,0:T(8,128)(2,1)S(1)}, bf16[64,3328]{1,0:T(8,128)(2,1)S(1)}, u32[]{:S(2)}, u32[]{:S(2)}) collective-permute-start(bf16[64,3328]{1,0:T(8,128)(2,1)S(1)} %collective-permute-done.10), channel_id=1, source_target_pairs={{0,4},{4,8},{8,12},{12,16},{16,20},{20,24},{24,28},{28,0},{1,5},{5... | collective-permute-start | bytes 1277960 | tf_op jit(solution)/shard_map/ppermute | solution.py:17
  77.4 6.0 %collective-permute-start.12 = (bf16[64,1664]{1,0:T(8,128)(2,1)S(1)}, bf16[64,1664]{1,0:T(8,128)(2,1)S(1)}, u32[]{:S(2)}, u32[]{:S(2)}) collective-permute-start(bf16[64,1664]{1,0:T(8,128)(2,1)S(1)} %slice.275), channel_id=1, source_target_pairs={{0,4},{4,8},{8,12},{12,16},{16,20},{20,24},{24,28},{28,0},{1,5},{5... | collective-permute-start | bytes 638984 | tf_op jit(solution)/shard_map/ppermute | solution.py:17
  77.6 6.4 %collective-permute-start.13 = (bf16[64,1664]{1,0:T(8,128)(2,1)S(1)}, bf16[64,1664]{1,0:T(8,128)(2,1)S(1)}, u32[]{:S(2)}, u32[]{:S(2)}) collective-permute-start(bf16[64,1664]{1,0:T(8,128)(2,1)S(1)} %slice.276), channel_id=1, source_target_pairs={{0,28},{4,0},{8,4},{12,8},{16,12},{20,16},{24,20},{28,24},{1,29},{... | collective-permute-start | bytes 638984 | tf_op jit(solution)/shard_map/ppermute | solution.py:17
  84.9 43.6 %copy-start.5 = (f32[128]{0:T(128)S(1)}, f32[128]{0:T(128)}, u32[]{:S(2)}) copy-start(f32[128]{0:T(128)} %param.8) | copy-start | bytes 1540
  89.8 38.7 %all-to-all-start = ((bf16[256,4,128]{2,1,0:T(4,128)(2,1)}), bf16[256,4,128]{2,1,0:T(4,128)(2,1)S(1)}, u32[]{:S(2)}, u32[]{:S(2)}) async-start(bf16[256,4,128]{2,1,0:T(4,128)(2,1)} %copy.13), calls=%async_computation | async-start | bytes 524288 | tf_op jit(solution)/shard_map/all_to_all | solution.py:71
  129.8 21.1 %all-to-all-start.1 = ((bf16[256,4,128]{2,1,0:T(4,128)(2,1)}), bf16[256,4,128]{2,1,0:T(4,128)(2,1)S(1)}, u32[]{:S(2)}, u32[]{:S(2)}) async-start(bf16[256,4,128]{2,1,0:T(4,128)(2,1)} %bitcast.8), calls=%async_computation.1 | async-start | bytes 524288 | tf_op jit(solution)/shard_map/all_to_all | solution.py:81
  (4 other events, 61.1 us)

commit v2 on v1

--- a/solution.py
+++ b/solution.py
@@ -17,37 +17,61 @@
     return lax.ppermute(value, axis, [(i, (i + step) % count) for i in range(count)])
 
 
-def ring(own, axis, count):
-    before, after = {0: own}, {0: own}
-    for k in range(1, count // 2):
-        before[-k] = shift(before[1 - k], axis, count, 1)
-        after[k] = shift(after[k - 1], axis, count, -1)
-    half = own.shape[1] // 256 * 128
-    far = jnp.concatenate(
-        [
-            shift(before[1 - count // 2][:, :half], axis, count, 1),
-            shift(after[count // 2 - 1][:, half:], axis, count, -1),
-        ],
-        axis=1,
-    )
-    return {k % count: v for k, v in {**before, **after, count // 2: far}.items()}
+def pair(before, after, axis, count):
+    return shift(before, axis, count, 1), shift(after, axis, count, -1)
+
+
+def halves(before, after, axis, count):
+    half = before.shape[1] // 256 * 128
+    return shift(before[:, :half], axis, count, 1), shift(after[:, half:], axis, count, -1)
+
+
+def tied(*values):
+    return lax.optimization_barrier(values)
 
 
 def gather_panel(own):
-    a, b = {}, {}
-    by_y = ring(own, "y", NY)
-    for dy, block in by_y.items():
-        b[dy, 0] = block[:, LA:]
-    along = ring(jnp.concatenate([by_y[dy][:, :LA] for dy in range(NY)], 0), "z", NZ)
-    for dz, block in along.items():
+    b0 = own[:, LA:]
+    b1 = pair(b0, b0, "z", NZ)
+    o1 = pair(own, own, "y", NY)
+    b2 = pair(*b1, "z", NZ)
+    o2 = halves(*o1, "y", NY)
+    *b2, o1a, o1b = tied(*b2, *o1)
+    o1 = (o1a, o1b)
+    b3 = pair(*b2, "z", NZ)
+    p0 = jnp.concatenate([b1[0], b1[1], b2[0], b2[1]], 0)
+    p1 = pair(p0, p0, "y", NY)
+    far = jnp.concatenate(tied(*o2), 1)
+    a0 = jnp.concatenate([v[:, :LA] for v in (own, o1[1], far, o1[0])], 0)
+    a1 = pair(a0, a0, "z", NZ)
+    b4 = jnp.concatenate(halves(*b3, "z", NZ), 1)
+    a2 = pair(*a1, "z", NZ)
+    q0 = jnp.concatenate([b3[0], b3[1], b4], 0)
+    *p1, a1a, a1b, q0 = tied(*p1, *a1, q0)
+    a1 = (a1a, a1b)
+    p2 = jnp.concatenate(halves(*p1, "y", NY), 1)
+    q1 = pair(q0, q0, "y", NY)
+    *a2, p1a, p1b = tied(*a2, *p1)
+    p1 = (p1a, p1b)
+    a3 = pair(*a2, "z", NZ)
+    *a3, p2 = tied(*a3, p2)
+    a4 = jnp.concatenate(halves(*a3, "z", NZ), 1)
+    q2 = jnp.concatenate(halves(*q1, "y", NY), 1)
+    by_z = (a0, a1[1], a2[1], a3[1], a4, a3[0], a2[0], a1[0])
+    a = {
+        (dy, dz): by_z[dz][dy * SHARE : (dy + 1) * SHARE]
+        for dy in range(NY)
+        for dz in range(NZ)
+    }
+    b = {}
+    for group, near in (
+        ((own[:, LA:], o1[1][:, LA:], far[:, LA:], o1[0][:, LA:]), (0,)),
+        ((p0, p1[1], p2, p1[0]), (7, 1, 6, 2)),
+        ((q0, q1[1], q2, q1[0]), (5, 3, 4)),
+    ):
         for dy in range(NY):
-            a[dy, dz] = block[dy * SHARE : (dy + 1) * SHARE]
-    by_z = ring(own[:, LA:], "z", NZ)
-    for near in ((7, 1, 6, 2), (5, 3, 4)):
-        group = ring(jnp.concatenate([by_z[dz] for dz in near], 0), "y", NY)
-        for dy, block in group.items():
             for n, dz in enumerate(near):
-                b[dy, dz] = block[n * SHARE : (n + 1) * SHARE]
+                b[dy, dz] = group[dy][n * SHARE : (n + 1) * SHARE]
     order = [(dy, dz) for dy in range(NY) for dz in range(NZ)]
     return jnp.concatenate(
         [jnp.concatenate([a[k], b[k]], 1) for k in order], 0

time: 161 us -> 145 us (0.901)
  waiting for transfers between devices: 74.9 us -> 59.4 us
    ppermute x28, waiting for transfers between devices: 45.5 us -> 30 us  [shift(): lax.ppermute(value, axis, [(i, (i + step) % count) for i in range(count)])]
    all_to_all x1, starting transfers between devices: 23.9 us -> 19.5 us  [local(): incoming = lax.all_to_all(outgoing, ALL, 0, 0, tiled=True)]
    ppermute x28, starting transfers between devices: 32.4 us -> 35.9 us  [shift(): lax.ppermute(value, axis, [(i, (i + step) % count) for i in range(count)])]
  transfers between devices with their start and end apart: 30 -> 30, of which waited for: 15 -> 10; matrix products, arithmetic and copies ran while one was open for 3% -> 3% of each run, Pallas kernels for 0% -> 0%
where the time goes in v2:
time: 145 us
  starting transfers between devices  61.7 us (43%)
  waiting for transfers between devices  59.4 us (41%)
  matrix products  10.7 us (7%)
  local copies, waits for them, and re-layouts  8.42 us (6%)
  other arithmetic  3.21 us (2%)
    ppermute x28, starting transfers between devices, shift(): lax.ppermute(value, axis, [(i, (i + step) % count) for i in range(count)])  35.9 us
    ppermute x28, waiting for transfers between devices, shift(): lax.ppermute(value, axis, [(i, (i + step) % count) for i in range(count)])  30 us
    all_to_all x1, starting transfers between devices, local(): incoming = lax.all_to_all(outgoing, ALL, 0, 0, tiled=True)  19.5 us
    all_to_all x1, waiting for transfers between devices, local(): back = lax.all_to_all(back, ALL, 0, 0, tiled=True)  14.8 us
    all_to_all x1, waiting for transfers between devices, local(): incoming = lax.all_to_all(outgoing, ALL, 0, 0, tiled=True)  14.5 us
    dot_general x1, matrix products, local(): lax.dot_general(whole, here, (((0,), (0,)), ((), ())), preferred_element_...  7.81 us
    all_to_all x1, starting transfers between devices, local(): back = lax.all_to_all(back, ALL, 0, 0, tiled=True)  6.23 us
  transfers between devices with their start and end apart: 30, of which 10 were waited for; matrix products, arithmetic and copies ran while one was open for 3% of the time, Pallas kernels for 0%

profile of v2, /device:TPU:1, one launch (start us, length us, event | category | flops | bytes accessed | tf_op | source)
XLA Modules:
  0.0 144.8 jit_solution(7030148373459560569)
XLA Ops:
  0.6 1.0 slice.278
  1.6 2.5 %collective-permute-start = (bf16[16,4864]{1,0:T(8,128)(2,1)S(1)}, bf16[16,4864]{1,0:T(8,128)(2,1)S(1)}, u32[]{:S(2)}, u32[]{:S(2)}) collective-permute-start(bf16[16,4864]{1,0:T(8,128)(2,1)S(1)} %slice.278), channel_id=1, source_target_pairs={{0,4},{4,8},{8,12},{12,16},{16,20},{20,24},{24,28},{28,0},{1,5},{5... | collective-permute-start | bytes 466952 | tf_op jit(solution)/shard_map/ppermute | solution.py:17
  4.1 4.0 %collective-permute-start.1 = (bf16[16,4864]{1,0:T(8,128)(2,1)S(1)}, bf16[16,4864]{1,0:T(8,128)(2,1)S(1)}, u32[]{:S(2)}, u32[]{:S(2)}) collective-permute-start(bf16[16,4864]{1,0:T(8,128)(2,1)S(1)} %slice.278), channel_id=1, source_target_pairs={{0,28},{4,0},{8,4},{12,8},{16,12},{20,16},{24,20},{28,24},{1,29},{... | collective-permute-start | bytes 466952 | tf_op jit(solution)/shard_map/ppermute | solution.py:17
  8.2 1.3 collective-permute-start.4
  9.5 1.4 collective-permute-start.5
  10.9 1.7 %constant_dynamic-update-slice_fusion.10 = bf16[512,8192]{1,0:T(8,128)(2,1)} fusion(bf16[8192,16]{0,1:T(8,128)(2,1)} %param.5), kind=kLoop, calls=%fused_computation.65 | loop fusion | bytes 524288
  12.6 0.9 slice.279
  13.6 2.7 %collective-permute-start.3 = (bf16[16,4864]{1,0:T(8,128)(2,1)S(1)}, bf16[16,4864]{1,0:T(8,128)(2,1)S(1)}, u32[]{:S(2)}, u32[]{:S(2)}) collective-permute-start(bf16[16,4864]{1,0:T(8,128)(2,1)S(1)} %collective-permute-done.1), channel_id=1, source_target_pairs={{0,28},{4,0},{8,4},{12,8},{16,12},{20,16},{24,20},{28,24},{1,29},{... | collective-permute-start | bytes 466952 | tf_op jit(solution)/shard_map/ppermute | solution.py:17
  16.7 2.7 %collective-permute-start.9 = (bf16[16,4096]{1,0:T(8,128)(2,1)S(1)}, bf16[16,4096]{1,0:T(8,128)(2,1)S(1)}, u32[]{:S(2)}, u32[]{:S(2)}) collective-permute-start(bf16[16,4096]{1,0:T(8,128)(2,1)S(1)} %slice.281), channel_id=1, source_target_pairs={{0,3},{1,0},{2,1},{3,2},{4,7},{5,4},{6,5},{7,6},{8,11},{9,8},{10,9... | collective-permute-start | bytes 393224 | tf_op jit(solution)/shard_map/ppermute | solution.py:17
  19.5 2.7 %collective-permute-start.13 = (bf16[16,4864]{1,0:T(8,128)(2,1)S(1)}, bf16[16,4864]{1,0:T(8,128)(2,1)S(1)}, u32[]{:S(2)}, u32[]{:S(2)}) collective-permute-start(bf16[16,4864]{1,0:T(8,128)(2,1)S(1)} %collective-permute-done.3), channel_id=1, source_target_pairs={{0,28},{4,0},{8,4},{12,8},{16,12},{20,16},{24,20},{28,24},{1,29},{... | collective-permute-start | bytes 466952 | tf_op jit(solution)/shard_map/ppermute | solution.py:17
  22.3 2.7 %collective-permute-start.7 = (bf16[64,4864]{1,0:T(8,128)(2,1)S(1)}, bf16[64,4864]{1,0:T(8,128)(2,1)S(1)}, u32[]{:S(2)}, u32[]{:S(2)}) collective-permute-start(bf16[64,4864]{1,0:T(8,128)(2,1)S(1)} %constant_dynamic-update-slice_fusion), channel_id=1, source_target_pairs={{0,3},{1,0},{2,1},{3,2},{4,7},{5,4},{6,5},{7,6},{8,11},{9,8},{10,9... | collective-permute-start | bytes 1867784 | tf_op jit(solution)/shard_map/ppermute | solution.py:17
  25.1 2.7 %collective-permute-start.15 = (bf16[16,2432]{1,0:T(8,128)(2,1)S(1)}, bf16[16,2432]{1,0:T(8,128)(2,1)S(1)}, u32[]{:S(2)}, u32[]{:S(2)}) collective-permute-start(bf16[16,2432]{1,0:T(8,128)(2,1)S(1)} %slice.283), channel_id=1, source_target_pairs={{0,28},{4,0},{8,4},{12,8},{16,12},{20,16},{24,20},{28,24},{1,29},{... | collective-permute-start | bytes 233480 | tf_op jit(solution)/shard_map/ppermute | solution.py:17
  28.0 1.9 %collective-permute-done.14 = bf16[16,2432]{1,0:T(8,128)(2,1)S(1)} collective-permute-done((bf16[16,2432]{1,0:T(8,128)(2,1)S(1)}, bf16[16,2432]{1,0:T(8,128)(2,1)S(1)}, u32[]{:S(2)}, u32[]{:S(2)}) %collective-permute-start.14) | collective-permute-done | bytes 77856 | tf_op jit(solution)/shard_map/ppermute | solution.py:17
  29.8 0.8 collective-permute-start.11
  30.7 7.4 %collective-permute-done.10 = bf16[64,3328]{1,0:T(8,128)(2,1)S(1)} collective-permute-done((bf16[64,3328]{1,0:T(8,128)(2,1)S(1)}, bf16[64,3328]{1,0:T(8,128)(2,1)S(1)}, u32[]{:S(2)}, u32[]{:S(2)}) %collective-permute-start.10) | collective-permute-done | bytes 426016 | tf_op jit(solution)/shard_map/ppermute | solution.py:17
  38.1 2.7 %collective-permute-start.17 = (bf16[64,3328]{1,0:T(8,128)(2,1)S(1)}, bf16[64,3328]{1,0:T(8,128)(2,1)S(1)}, u32[]{:S(2)}, u32[]{:S(2)}) collective-permute-start(bf16[64,3328]{1,0:T(8,128)(2,1)S(1)} %collective-permute-done.11), channel_id=1, source_target_pairs={{0,28},{4,0},{8,4},{12,8},{16,12},{20,16},{24,20},{28,24},{1,29},{... | collective-permute-start | bytes 1277960 | tf_op jit(solution)/shard_map/ppermute | solution.py:17
  40.8 1.5 %collective-permute-start.24 = (bf16[48,4864]{1,0:T(8,128)(2,1)S(1)}, bf16[48,4864]{1,0:T(8,128)(2,1)S(1)}, u32[]{:S(2)}, u32[]{:S(2)}) collective-permute-start(bf16[48,4864]{1,0:T(8,128)(2,1)S(1)} %maximum_maximum_fusion), channel_id=1, source_target_pairs={{0,3},{1,0},{2,1},{3,2},{4,7},{5,4},{6,5},{7,6},{8,11},{9,8},{10,9... | collective-permute-start | bytes 1400840 | tf_op jit(solution)/shard_map/ppermute | solution.py:17
  43.3 3.0 %collective-permute-done.16 = bf16[64,3328]{1,0:T(8,128)(2,1)S(1)} collective-permute-done((bf16[64,3328]{1,0:T(8,128)(2,1)S(1)}, bf16[64,3328]{1,0:T(8,128)(2,1)S(1)}, u32[]{:S(2)}, u32[]{:S(2)}) %collective-permute-start.16) | collective-permute-done | bytes 426016 | tf_op jit(solution)/shard_map/ppermute | solution.py:17
  46.2 1.7 %collective-permute-start.21 = (bf16[64,2432]{1,0:T(8,128)(2,1)S(1)}, bf16[64,2432]{1,0:T(8,128)(2,1)S(1)}, u32[]{:S(2)}, u32[]{:S(2)}) collective-permute-start(bf16[64,2432]{1,0:T(8,128)(2,1)S(1)} %slice.222), channel_id=1, source_target_pairs={{0,3},{1,0},{2,1},{3,2},{4,7},{5,4},{6,5},{7,6},{8,11},{9,8},{10,9... | collective-permute-start | bytes 933896 | tf_op jit(solution)/shard_map/ppermute | solution.py:17
  48.9 8.2 %collective-permute-done.20 = bf16[64,2432]{1,0:T(8,128)(2,1)S(1)} collective-permute-done((bf16[64,2432]{1,0:T(8,128)(2,1)S(1)}, bf16[64,2432]{1,0:T(8,128)(2,1)S(1)}, u32[]{:S(2)}, u32[]{:S(2)}) %collective-permute-start.20) | collective-permute-done | bytes 311328 | tf_op jit(solution)/shard_map/ppermute | solution.py:17
  57.6 2.7 %collective-permute-start.27 = (bf16[48,2432]{1,0:T(8,128)(2,1)S(1)}, bf16[48,2432]{1,0:T(8,128)(2,1)S(1)}, u32[]{:S(2)}, u32[]{:S(2)}) collective-permute-start(bf16[48,2432]{1,0:T(8,128)(2,1)S(1)} %slice.290), channel_id=1, source_target_pairs={{0,3},{1,0},{2,1},{3,2},{4,7},{5,4},{6,5},{7,6},{8,11},{9,8},{10,9... | collective-permute-start | bytes 700424 | tf_op jit(solution)/shard_map/ppermute | solution.py:17
  60.4 4.7 %collective-permute-done.26 = bf16[48,2432]{1,0:T(8,128)(2,1)S(1)} collective-permute-done((bf16[48,2432]{1,0:T(8,128)(2,1)S(1)}, bf16[48,2432]{1,0:T(8,128)(2,1)S(1)}, u32[]{:S(2)}, u32[]{:S(2)}) %collective-permute-start.26) | collective-permute-done | bytes 233504 | tf_op jit(solution)/shard_map/ppermute | solution.py:17
  65.4 2.7 %collective-permute-start.23 = (bf16[64,1664]{1,0:T(8,128)(2,1)S(1)}, bf16[64,1664]{1,0:T(8,128)(2,1)S(1)}, u32[]{:S(2)}, u32[]{:S(2)}) collective-permute-start(bf16[64,1664]{1,0:T(8,128)(2,1)S(1)} %slice.226), channel_id=1, source_target_pairs={{0,28},{4,0},{8,4},{12,8},{16,12},{20,16},{24,20},{28,24},{1,29},{... | collective-permute-start | bytes 638984 | tf_op jit(solution)/shard_map/ppermute | solution.py:17
  68.1 3.4 %collective-permute-done.22 = bf16[64,1664]{1,0:T(8,128)(2,1)S(1)} collective-permute-done((bf16[64,1664]{1,0:T(8,128)(2,1)S(1)}, bf16[64,1664]{1,0:T(8,128)(2,1)S(1)}, u32[]{:S(2)}, u32[]{:S(2)}) %collective-permute-start.22) | collective-permute-done | bytes 213024 | tf_op jit(solution)/shard_map/ppermute | solution.py:17
  71.6 1.3 collective-permute-done.23
  73.8 2.3 %fusion.24 = bf16[512,256]{1,0:T(8,128)(2,1)S(1)} fusion(bf16[512,8192]{1,0:T(8,128)(2,1)S(1)} %maximum_dynamic-update-slice_fusion, bf16[8192,256]{1,0:T(8,128)(2,1)S(1)} %copy-done.4), kind=kOutput, calls=%fused_computation.83 | convolution fusion | flops 2147483648 | bytes 12845056 | tf_op jit(solution)/shard_map/dot_general | solution.py:91
  77.7 0.9 copy.13
  78.6 19.5 %all-to-all-start = ((bf16[256,4,128]{2,1,0:T(4,128)(2,1)}), bf16[256,4,128]{2,1,0:T(4,128)(2,1)S(1)}, u32[]{:S(2)}, u32[]{:S(2)}) async-start(bf16[256,4,128]{2,1,0:T(4,128)(2,1)} %copy.13), calls=%async_computation | async-start | bytes 524288 | tf_op jit(solution)/shard_map/all_to_all | solution.py:95
  98.4 14.5 %all-to-all-done = bf16[256,4,128]{2,1,0:T(4,128)(2,1)S(1)} async-done(((bf16[256,4,128]{2,1,0:T(4,128)(2,1)}), bf16[256,4,128]{2,1,0:T(4,128)(2,1)S(1)}, u32[]{:S(2)}, u32[]{:S(2)}) %all-to-all-start) | async-done | bytes 262176 | tf_op jit(solution)/shard_map/all_to_all | solution.py:95
  114.3 6.2 %all-to-all-start.1 = ((bf16[256,4,128]{2,1,0:T(4,128)(2,1)}), bf16[256,4,128]{2,1,0:T(4,128)(2,1)S(1)}, u32[]{:S(2)}, u32[]{:S(2)}) async-start(bf16[256,4,128]{2,1,0:T(4,128)(2,1)} %bitcast.8), calls=%async_computation.1 | async-start | bytes 524288 | tf_op jit(solution)/shard_map/all_to_all | solution.py:105
  120.6 14.8 %all-to-all-done.1 = bf16[256,4,128]{2,1,0:T(4,128)(2,1)S(1)} async-done(((bf16[256,4,128]{2,1,0:T(4,128)(2,1)}), bf16[256,4,128]{2,1,0:T(4,128)(2,1)S(1)}, u32[]{:S(2)}, u32[]{:S(2)}) %all-to-all-start.1) | async-done | bytes 262176 | tf_op jit(solution)/shard_map/all_to_all | solution.py:105
  136.4 7.8 %convolution_convert_fusion = bf16[8192,256]{1,0:T(8,128)(2,1)} fusion(bf16[512,8192]{1,0:T(8,128)(2,1)} %copy-done.2, bf16[512,256]{1,0:T(8,128)(2,1)S(1)} %bitcast.42), kind=kOutput, calls=%fused_computation | convolution fusion | flops 2149580800 | bytes 12845056 | tf_op jit(solution)/shard_map/dot_general | solution.py:111
  (130 shorter events, 9.0 us)
Async XLA Ops:
  0.6 112.3 %copy-start = (f32[128,128]{1,0:T(8,128)S(1)}, f32[128,128]{1,0:T(8,128)}, u32[]{:S(2)}) copy-start(f32[128,128]{1,0:T(8,128)} %param.9) | copy-start | bytes 196612
  1.6 11.9 %collective-permute-start = (bf16[16,4864]{1,0:T(8,128)(2,1)S(1)}, bf16[16,4864]{1,0:T(8,128)(2,1)S(1)}, u32[]{:S(2)}, u32[]{:S(2)}) collective-permute-start(bf16[16,4864]{1,0:T(8,128)(2,1)S(1)} %slice.278), channel_id=1, source_target_pairs={{0,4},{4,8},{8,12},{12,16},{16,20},{20,24},{24,28},{28,0},{1,5},{5... | collective-permute-start | bytes 466952 | tf_op jit(solution)/shard_map/ppermute | solution.py:17
  4.1 9.5 %collective-permute-start.1 = (bf16[16,4864]{1,0:T(8,128)(2,1)S(1)}, bf16[16,4864]{1,0:T(8,128)(2,1)S(1)}, u32[]{:S(2)}, u32[]{:S(2)}) collective-permute-start(bf16[16,4864]{1,0:T(8,128)(2,1)S(1)} %slice.278), channel_id=1, source_target_pairs={{0,28},{4,0},{8,4},{12,8},{16,12},{20,16},{24,20},{28,24},{1,29},{... | collective-permute-start | bytes 466952 | tf_op jit(solution)/shard_map/ppermute | solution.py:17
  8.2 8.4 %collective-permute-start.4 = (bf16[16,8192]{1,0:T(8,128)(2,1)}, bf16[16,8192]{1,0:T(8,128)(2,1)S(1)}, u32[]{:S(2)}, u32[]{:S(2)}) collective-permute-start(bf16[16,8192]{1,0:T(8,128)(2,1)} %bitcast.39), channel_id=1, source_target_pairs={{0,1},{1,2},{2,3},{3,0},{4,5},{5,6},{6,7},{7,4},{8,9},{9,10},{10,1... | collective-permute-start | bytes 786440 | tf_op jit(solution)/shard_map/ppermute | solution.py:17
  9.5 7.2 %collective-permute-start.5 = (bf16[16,8192]{1,0:T(8,128)(2,1)}, bf16[16,8192]{1,0:T(8,128)(2,1)S(1)}, u32[]{:S(2)}, u32[]{:S(2)}) collective-permute-start(bf16[16,8192]{1,0:T(8,128)(2,1)} %bitcast.40), channel_id=1, source_target_pairs={{0,3},{1,0},{2,1},{3,2},{4,7},{5,4},{6,5},{7,6},{8,11},{9,8},{10,9... | collective-permute-start | bytes 786440 | tf_op jit(solution)/shard_map/ppermute | solution.py:17
  13.5 5.9 %collective-permute-start.2 = (bf16[16,4864]{1,0:T(8,128)(2,1)S(1)}, bf16[16,4864]{1,0:T(8,128)(2,1)S(1)}, u32[]{:S(2)}, u32[]{:S(2)}) collective-permute-start(bf16[16,4864]{1,0:T(8,128)(2,1)S(1)} %collective-permute-done), channel_id=1, source_target_pairs={{0,4},{4,8},{8,12},{12,16},{16,20},{20,24},{24,28},{28,0},{1,5},{5... | collective-permute-start | bytes 466952 | tf_op jit(solution)/shard_map/ppermute | solution.py:17
  13.6 5.8 %collective-permute-start.3 = (bf16[16,4864]{1,0:T(8,128)(2,1)S(1)}, bf16[16,4864]{1,0:T(8,128)(2,1)S(1)}, u32[]{:S(2)}, u32[]{:S(2)}) collective-permute-start(bf16[16,4864]{1,0:T(8,128)(2,1)S(1)} %collective-permute-done.1), channel_id=1, source_target_pairs={{0,28},{4,0},{8,4},{12,8},{16,12},{20,16},{24,20},{28,24},{1,29},{... | collective-permute-start | bytes 466952 | tf_op jit(solution)/shard_map/ppermute | solution.py:17
  16.6 5.7 %collective-permute-start.8 = (bf16[16,4096]{1,0:T(8,128)(2,1)S(1)}, bf16[16,4096]{1,0:T(8,128)(2,1)S(1)}, u32[]{:S(2)}, u32[]{:S(2)}) collective-permute-start(bf16[16,4096]{1,0:T(8,128)(2,1)S(1)} %slice.280), channel_id=1, source_target_pairs={{0,1},{1,2},{2,3},{3,0},{4,5},{5,6},{6,7},{7,4},{8,9},{9,10},{10,1... | collective-permute-start | bytes 393224 | tf_op jit(solution)/shard_map/ppermute | solution.py:17
  16.7 8.2 %collective-permute-start.9 = (bf16[16,4096]{1,0:T(8,128)(2,1)S(1)}, bf16[16,4096]{1,0:T(8,128)(2,1)S(1)}, u32[]{:S(2)}, u32[]{:S(2)}) collective-permute-start(bf16[16,4096]{1,0:T(8,128)(2,1)S(1)} %slice.281), channel_id=1, source_target_pairs={{0,3},{1,0},{2,1},{3,2},{4,7},{5,4},{6,5},{7,6},{8,11},{9,8},{10,9... | collective-permute-start | bytes 393224 | tf_op jit(solution)/shard_map/ppermute | solution.py:17
  19.5 5.5 %collective-permute-start.12 = (bf16[16,4864]{1,0:T(8,128)(2,1)S(1)}, bf16[16,4864]{1,0:T(8,128)(2,1)S(1)}, u32[]{:S(2)}, u32[]{:S(2)}) collective-permute-start(bf16[16,4864]{1,0:T(8,128)(2,1)S(1)} %collective-permute-done.2), channel_id=1, source_target_pairs={{0,4},{4,8},{8,12},{12,16},{16,20},{20,24},{24,28},{28,0},{1,5},{5... | collective-permute-start | bytes 466952 | tf_op jit(solution)/shard_map/ppermute | solution.py:17
  19.5 5.6 %collective-permute-start.13 = (bf16[16,4864]{1,0:T(8,128)(2,1)S(1)}, bf16[16,4864]{1,0:T(8,128)(2,1)S(1)}, u32[]{:S(2)}, u32[]{:S(2)}) collective-permute-start(bf16[16,4864]{1,0:T(8,128)(2,1)S(1)} %collective-permute-done.3), channel_id=1, source_target_pairs={{0,28},{4,0},{8,4},{12,8},{16,12},{20,16},{24,20},{28,24},{1,29},{... | collective-permute-start | bytes 466952 | tf_op jit(solution)/shard_map/ppermute | solution.py:17
  22.2 18.5 %collective-permute-start.6 = (bf16[64,4864]{1,0:T(8,128)(2,1)S(1)}, bf16[64,4864]{1,0:T(8,128)(2,1)S(1)}, u32[]{:S(2)}, u32[]{:S(2)}) collective-permute-start(bf16[64,4864]{1,0:T(8,128)(2,1)S(1)} %constant_dynamic-update-slice_fusion), channel_id=1, source_target_pairs={{0,1},{1,2},{2,3},{3,0},{4,5},{5,6},{6,7},{7,4},{8,9},{9,10},{10,1... | collective-permute-start | bytes 1867784 | tf_op jit(solution)/shard_map/ppermute | solution.py:17
  22.3 18.4 %collective-permute-start.7 = (bf16[64,4864]{1,0:T(8,128)(2,1)S(1)}, bf16[64,4864]{1,0:T(8,128)(2,1)S(1)}, u32[]{:S(2)}, u32[]{:S(2)}) collective-permute-start(bf16[64,4864]{1,0:T(8,128)(2,1)S(1)} %constant_dynamic-update-slice_fusion), channel_id=1, source_target_pairs={{0,3},{1,0},{2,1},{3,2},{4,7},{5,4},{6,5},{7,6},{8,11},{9,8},{10,9... | collective-permute-start | bytes 1867784 | tf_op jit(solution)/shard_map/ppermute | solution.py:17
  25.0 4.8 %collective-permute-start.14 = (bf16[16,2432]{1,0:T(8,128)(2,1)S(1)}, bf16[16,2432]{1,0:T(8,128)(2,1)S(1)}, u32[]{:S(2)}, u32[]{:S(2)}) collective-permute-start(bf16[16,2432]{1,0:T(8,128)(2,1)S(1)} %slice.282), channel_id=1, source_target_pairs={{0,4},{4,8},{8,12},{12,16},{16,20},{20,24},{24,28},{28,0},{1,5},{5... | collective-permute-start | bytes 233480 | tf_op jit(solution)/shard_map/ppermute | solution.py:17
  25.1 5.5 %collective-permute-start.15 = (bf16[16,2432]{1,0:T(8,128)(2,1)S(1)}, bf16[16,2432]{1,0:T(8,128)(2,1)S(1)}, u32[]{:S(2)}, u32[]{:S(2)}) collective-permute-start(bf16[16,2432]{1,0:T(8,128)(2,1)S(1)} %slice.283), channel_id=1, source_target_pairs={{0,28},{4,0},{8,4},{12,8},{16,12},{20,16},{24,20},{28,24},{1,29},{... | collective-permute-start | bytes 233480 | tf_op jit(solution)/shard_map/ppermute | solution.py:17
  27.9 10.2 %collective-permute-start.10 = (bf16[64,3328]{1,0:T(8,128)(2,1)S(1)}, bf16[64,3328]{1,0:T(8,128)(2,1)S(1)}, u32[]{:S(2)}, u32[]{:S(2)}) collective-permute-start(bf16[64,3328]{1,0:T(8,128)(2,1)S(1)} %pad_maximum_fusion.1), channel_id=1, source_target_pairs={{0,4},{4,8},{8,12},{12,16},{16,20},{20,24},{24,28},{28,0},{1,5},{5... | collective-permute-start | bytes 1277960 | tf_op jit(solution)/shard_map/ppermute | solution.py:17
  29.8 8.2 %collective-permute-start.11 = (bf16[64,3328]{1,0:T(8,128)(2,1)S(1)}, bf16[64,3328]{1,0:T(8,128)(2,1)S(1)}, u32[]{:S(2)}, u32[]{:S(2)}) collective-permute-start(bf16[64,3328]{1,0:T(8,128)(2,1)S(1)} %pad_maximum_fusion.1), channel_id=1, source_target_pairs={{0,28},{4,0},{8,4},{12,8},{16,12},{20,16},{24,20},{28,24},{1,29},{... | collective-permute-start | bytes 1277960 | tf_op jit(solution)/shard_map/ppermute | solution.py:17
  38.1 8.2 %collective-permute-start.16 = (bf16[64,3328]{1,0:T(8,128)(2,1)S(1)}, bf16[64,3328]{1,0:T(8,128)(2,1)S(1)}, u32[]{:S(2)}, u32[]{:S(2)}) collective-permute-start(bf16[64,3328]{1,0:T(8,128)(2,1)S(1)} %collective-permute-done.10), channel_id=1, source_target_pairs={{0,4},{4,8},{8,12},{12,16},{16,20},{20,24},{24,28},{28,0},{1,5},{5... | collective-permute-start | bytes 1277960 | tf_op jit(solution)/shard_map/ppermute | solution.py:17
  38.1 9.9 %collective-permute-start.17 = (bf16[64,3328]{1,0:T(8,128)(2,1)S(1)}, bf16[64,3328]{1,0:T(8,128)(2,1)S(1)}, u32[]{:S(2)}, u32[]{:S(2)}) collective-permute-start(bf16[64,3328]{1,0:T(8,128)(2,1)S(1)} %collective-permute-done.11), channel_id=1, source_target_pairs={{0,28},{4,0},{8,4},{12,8},{16,12},{20,16},{24,20},{28,24},{1,29},{... | collective-permute-start | bytes 1277960 | tf_op jit(solution)/shard_map/ppermute | solution.py:17
  40.8 16.7 %collective-permute-start.24 = (bf16[48,4864]{1,0:T(8,128)(2,1)S(1)}, bf16[48,4864]{1,0:T(8,128)(2,1)S(1)}, u32[]{:S(2)}, u32[]{:S(2)}) collective-permute-start(bf16[48,4864]{1,0:T(8,128)(2,1)S(1)} %maximum_maximum_fusion), channel_id=1, source_target_pairs={{0,3},{1,0},{2,1},{3,2},{4,7},{5,4},{6,5},{7,6},{8,11},{9,8},{10,9... | collective-permute-start | bytes 1400840 | tf_op jit(solution)/shard_map/ppermute | solution.py:17
  42.2 15.2 %collective-permute-start.25 = (bf16[48,4864]{1,0:T(8,128)(2,1)S(1)}, bf16[48,4864]{1,0:T(8,128)(2,1)S(1)}, u32[]{:S(2)}, u32[]{:S(2)}) collective-permute-start(bf16[48,4864]{1,0:T(8,128)(2,1)S(1)} %maximum_maximum_fusion), channel_id=1, source_target_pairs={{0,1},{1,2},{2,3},{3,0},{4,5},{5,6},{6,7},{7,4},{8,9},{9,10},{10,1... | collective-permute-start | bytes 1400840 | tf_op jit(solution)/shard_map/ppermute | solution.py:17
  42.3 14.7 %collective-permute-start.20 = (bf16[64,2432]{1,0:T(8,128)(2,1)S(1)}, bf16[64,2432]{1,0:T(8,128)(2,1)S(1)}, u32[]{:S(2)}, u32[]{:S(2)}) collective-permute-start(bf16[64,2432]{1,0:T(8,128)(2,1)S(1)} %slice.221), channel_id=1, source_target_pairs={{0,1},{1,2},{2,3},{3,0},{4,5},{5,6},{6,7},{7,4},{8,9},{9,10},{10,1... | collective-permute-start | bytes 933896 | tf_op jit(solution)/shard_map/ppermute | solution.py:17
  46.2 11.1 %collective-permute-start.21 = (bf16[64,2432]{1,0:T(8,128)(2,1)S(1)}, bf16[64,2432]{1,0:T(8,128)(2,1)S(1)}, u32[]{:S(2)}, u32[]{:S(2)}) collective-permute-start(bf16[64,2432]{1,0:T(8,128)(2,1)S(1)} %slice.222), channel_id=1, source_target_pairs={{0,3},{1,0},{2,1},{3,2},{4,7},{5,4},{6,5},{7,6},{8,11},{9,8},{10,9... | collective-permute-start | bytes 933896 | tf_op jit(solution)/shard_map/ppermute | solution.py:17
  48.0 17.2 %collective-permute-start.18 = (bf16[64,3328]{1,0:T(8,128)(2,1)S(1)}, bf16[64,3328]{1,0:T(8,128)(2,1)S(1)}, u32[]{:S(2)}, u32[]{:S(2)}) collective-permute-start(bf16[64,3328]{1,0:T(8,128)(2,1)S(1)} %collective-permute-done.16), channel_id=1, source_target_pairs={{0,4},{4,8},{8,12},{12,16},{16,20},{20,24},{24,28},{28,0},{1,5},{5... | collective-permute-start | bytes 1277960 | tf_op jit(solution)/shard_map/ppermute | solution.py:17
  57.0 8.1 %collective-permute-start.19 = (bf16[64,3328]{1,0:T(8,128)(2,1)S(1)}, bf16[64,3328]{1,0:T(8,128)(2,1)S(1)}, u32[]{:S(2)}, u32[]{:S(2)}) collective-permute-start(bf16[64,3328]{1,0:T(8,128)(2,1)S(1)} %collective-permute-done.17), channel_id=1, source_target_pairs={{0,28},{4,0},{8,4},{12,8},{16,12},{20,16},{24,20},{28,24},{1,29},{... | collective-permute-start | bytes 1277960 | tf_op jit(solution)/shard_map/ppermute | solution.py:17
  57.4 7.6 %collective-permute-start.26 = (bf16[48,2432]{1,0:T(8,128)(2,1)S(1)}, bf16[48,2432]{1,0:T(8,128)(2,1)S(1)}, u32[]{:S(2)}, u32[]{:S(2)}) collective-permute-start(bf16[48,2432]{1,0:T(8,128)(2,1)S(1)} %slice.289), channel_id=1, source_target_pairs={{0,1},{1,2},{2,3},{3,0},{4,5},{5,6},{6,7},{7,4},{8,9},{9,10},{10,1... | collective-permute-start | bytes 700424 | tf_op jit(solution)/shard_map/ppermute | solution.py:17
  57.6 7.5 %collective-permute-start.27 = (bf16[48,2432]{1,0:T(8,128)(2,1)S(1)}, bf16[48,2432]{1,0:T(8,128)(2,1)S(1)}, u32[]{:S(2)}, u32[]{:S(2)}) collective-permute-start(bf16[48,2432]{1,0:T(8,128)(2,1)S(1)} %slice.290), channel_id=1, source_target_pairs={{0,3},{1,0},{2,1},{3,2},{4,7},{5,4},{6,5},{7,6},{8,11},{9,8},{10,9... | collective-permute-start | bytes 700424 | tf_op jit(solution)/shard_map/ppermute | solution.py:17
  65.3 6.3 %collective-permute-start.22 = (bf16[64,1664]{1,0:T(8,128)(2,1)S(1)}, bf16[64,1664]{1,0:T(8,128)(2,1)S(1)}, u32[]{:S(2)}, u32[]{:S(2)}) collective-permute-start(bf16[64,1664]{1,0:T(8,128)(2,1)S(1)} %slice.225), channel_id=1, source_target_pairs={{0,4},{4,8},{8,12},{12,16},{16,20},{20,24},{24,28},{28,0},{1,5},{5... | collective-permute-start | bytes 638984 | tf_op jit(solution)/shard_map/ppermute | solution.py:17
  65.4 7.5 %collective-permute-start.23 = (bf16[64,1664]{1,0:T(8,128)(2,1)S(1)}, bf16[64,1664]{1,0:T(8,128)(2,1)S(1)}, u32[]{:S(2)}, u32[]{:S(2)}) collective-permute-start(bf16[64,1664]{1,0:T(8,128)(2,1)S(1)} %slice.226), channel_id=1, source_target_pairs={{0,28},{4,0},{8,4},{12,8},{16,12},{20,16},{24,20},{28,24},{1,29},{... | collective-permute-start | bytes 638984 | tf_op jit(solution)/shard_map/ppermute | solution.py:17
  73.8 39.2 %copy-start.5 = (f32[128]{0:T(128)S(1)}, f32[128]{0:T(128)}, u32[]{:S(2)}) copy-start(f32[128]{0:T(128)} %param.8) | copy-start | bytes 1540
  78.6 34.2 %all-to-all-start = ((bf16[256,4,128]{2,1,0:T(4,128)(2,1)}), bf16[256,4,128]{2,1,0:T(4,128)(2,1)S(1)}, u32[]{:S(2)}, u32[]{:S(2)}) async-start(bf16[256,4,128]{2,1,0:T(4,128)(2,1)} %copy.13), calls=%async_computation | async-start | bytes 524288 | tf_op jit(solution)/shard_map/all_to_all | solution.py:95
  114.3 21.1 %all-to-all-start.1 = ((bf16[256,4,128]{2,1,0:T(4,128)(2,1)}), bf16[256,4,128]{2,1,0:T(4,128)(2,1)S(1)}, u32[]{:S(2)}, u32[]{:S(2)}) async-start(bf16[256,4,128]{2,1,0:T(4,128)(2,1)} %bitcast.8), calls=%async_computation.1 | async-start | bytes 524288 | tf_op jit(solution)/shard_map/all_to_all | solution.py:105
  (4 other events, 52.5 us)

commit v3 on v2

--- a/solution.py
+++ b/solution.py
@@ -6,6 +6,7 @@
 ROW = ("x", "core")
 COL = ("z", "y")
 ALL = ROW + COL
+CHIPS = ("x",) + COL
 NX, NC, NZ, NY = 4, 2, 8, 4
 SHARE = 16
 TRAITS = 128
@@ -86,28 +87,38 @@
 
 def local(panel, pheno, kin_values, trait_values, trait_basis):
     z, y = lax.axis_index("z"), lax.axis_index("y")
-    row = lax.axis_index("x") * NC + lax.axis_index("core")
+    core = lax.axis_index("core")
+    row = lax.axis_index("x") * NC + core
     whole = gather_panel(panel.T)
     part = jnp.dot(whole, pheno, preferred_element_type=jnp.float32)
     part = part.reshape(NY, NZ, SHARE, TRAITS // 32 * SETS)
-    part = turn(turn(part, 1, z), 0, y).reshape(NY, 128, 4, SETS)
-    outgoing = part.astype(jnp.bfloat16).transpose(3, 0, 2, 1).reshape(256, 4, 128)
-    incoming = lax.all_to_all(outgoing, ALL, 0, 0, tiled=True)
-    summed = jnp.sum(incoming.reshape(8, TRAITS, 128).astype(jnp.float32), 0)
-    kin = lax.dynamic_index_in_dim(kin_values.reshape(NZ, NY, SHARE), y, 1, False)
+    part = turn(part, 1, z)
+    part = jnp.concatenate([part, part], 0)
+    mine = lax.dynamic_slice_in_dim(part, (NC * core + NY - y) % NY, NC, 0)
+    theirs = lax.dynamic_slice_in_dim(part, (NC * (1 - core) + NY - y) % NY, NC, 0)
+    part = mine + shift(theirs, "core", NC, 1)
+    part = part.reshape(NC, 128, 4, SETS)
+    outgoing = part.astype(jnp.bfloat16).transpose(3, 0, 2, 1).reshape(128, 4, 128)
+    incoming = lax.all_to_all(outgoing, CHIPS, 0, 0, tiled=True)
+    summed = jnp.sum(incoming.reshape(NX, TRAITS, 128).astype(jnp.float32), 0)
+    kin = lax.dynamic_index_in_dim(
+        kin_values.reshape(NZ, NY, SHARE), NC * core + y % NC, 1, False
+    )
     gain = trait_values[:, None] * kin.reshape(1, 128)
     high = lax.Precision.HIGHEST
     rotated = jnp.einsum("tj,tp->jp", trait_basis, summed, precision=high)
     scaled = rotated * (gain / (gain + 1.0))
     unrotated = jnp.einsum("tj,jp->tp", trait_basis, scaled, precision=high)
     low = unrotated.astype(jnp.bfloat16).reshape(1, 32, 4, 128)
-    back = jnp.broadcast_to(low, (8, 32, 4, 128)).reshape(256, 4, 128)
-    back = lax.all_to_all(back, ALL, 0, 0, tiled=True)
-    coeffs_low = back.reshape(SETS, NY, 4, 128).transpose(1, 3, 2, 0)
+    back = jnp.broadcast_to(low, (NX, 32, 4, 128)).reshape(128, 4, 128)
+    back = lax.all_to_all(back, CHIPS, 0, 0, tiled=True)
+    coeffs_low = back.reshape(SETS, NC, 4, 128).transpose(1, 3, 2, 0).reshape(256, 256)
+    coeffs_low = jnp.concatenate([coeffs_low, shift(coeffs_low, "core", NC, 1)], 0)
     coeffs_low = coeffs_low.reshape(NY, NZ, SHARE, 256)
     coeffs = lax.dynamic_index_in_dim(coeffs_low, row, 1, False)
-    coeffs = coeffs.reshape(NY * SHARE, 256).astype(jnp.float32)
-    here = turn(turn(coeffs_low, 1, (NZ - z) % NZ), 0, (NY - y) % NY).reshape(512, 256)
+    coeffs = turn(coeffs, 0, NC * core).reshape(NY * SHARE, 256).astype(jnp.float32)
+    here = turn(coeffs_low, 1, (NZ - z) % NZ)
+    here = turn(here, 0, (NC * core + NY - y) % NY).reshape(512, 256)
     genetic = lax.dot_general(
         whole, here, (((0,), (0,)), ((), ())), preferred_element_type=jnp.float32
     )

time: 145 us -> 142 us (0.979)
  blocking collectives: 0 us -> 17 us
  waiting for transfers between devices: 59.4 us -> 42.9 us
  starting transfers between devices: 61.7 us -> 60 us
  local copies, waits for them, and re-layouts: 8.42 us -> 6.78 us
    all_to_all x2 -> x1, waiting for transfers between devices: 29.4 us -> 10.7 us  [local(): incoming = lax.all_to_all(outgoing, CHIPS, 0, 0, tiled=True)]
    all_to_all x0 -> x1, blocking collectives: none -> 17 us  [local(): back = lax.all_to_all(back, CHIPS, 0, 0, tiled=True)]
    all_to_all x2 -> x1, starting transfers between devices: 25.7 us -> 11.5 us  [local(): incoming = lax.all_to_all(outgoing, CHIPS, 0, 0, tiled=True)]
    ppermute x28 -> x30, starting transfers between devices: 35.9 us -> 48.5 us  [shift(): lax.ppermute(value, axis, [(i, (i + step) % count) for i in range(count)])]
    ppermute x28 -> x30, waiting for transfers between devices: 30 us -> 32.2 us  [shift(): lax.ppermute(value, axis, [(i, (i + step) % count) for i in range(count)])]
  transfers between devices with their start and end apart: 30 -> 31, of which waited for: 10 -> 11; matrix products, arithmetic and copies ran while one was open for 3% -> 4% of each run, Pallas kernels for 0% -> 0%
where the time goes in v3:
time: 142 us
  starting transfers between devices  60 us (42%)
  waiting for transfers between devices  42.9 us (30%)
  blocking collectives  17 us (12%)
  matrix products  10.7 us (8%)
  local copies, waits for them, and re-layouts  6.78 us (5%)
  other arithmetic  3.28 us (2%)
  between operations  1.44 us (1%)
    ppermute x30, starting transfers between devices, shift(): lax.ppermute(value, axis, [(i, (i + step) % count) for i in range(count)])  48.5 us
    ppermute x30, waiting for transfers between devices, shift(): lax.ppermute(value, axis, [(i, (i + step) % count) for i in range(count)])  32.2 us
    all_to_all x1, blocking collectives, local(): back = lax.all_to_all(back, CHIPS, 0, 0, tiled=True)  17 us
    all_to_all x1, starting transfers between devices, local(): incoming = lax.all_to_all(outgoing, CHIPS, 0, 0, tiled=True)  11.5 us
    all_to_all x1, waiting for transfers between devices, local(): incoming = lax.all_to_all(outgoing, CHIPS, 0, 0, tiled=True)  10.7 us
    dot_general x1, matrix products, local(): lax.dot_general(whole, here, (((0,), (0,)), ((), ())), preferred_element_...  7.81 us
  transfers between devices with their start and end apart: 31, of which 11 were waited for; matrix products, arithmetic and copies ran while one was open for 4% of the time, Pallas kernels for 0%

profile of v3, /device:TPU:1, one launch (start us, length us, event | category | flops | bytes accessed | tf_op | source)
XLA Modules:
  0.0 142.1 jit_solution(10628218546185129945)
XLA Ops:
  0.6 1.0 slice.278
  1.6 2.5 %collective-permute-start = (bf16[16,4864]{1,0:T(8,128)(2,1)S(1)}, bf16[16,4864]{1,0:T(8,128)(2,1)S(1)}, u32[]{:S(2)}, u32[]{:S(2)}) collective-permute-start(bf16[16,4864]{1,0:T(8,128)(2,1)S(1)} %slice.278), channel_id=1, source_target_pairs={{0,4},{4,8},{8,12},{12,16},{16,20},{20,24},{24,28},{28,0},{1,5},{5... | collective-permute-start | bytes 466952 | tf_op jit(solution)/shard_map/ppermute | solution.py:18
  4.1 4.0 %collective-permute-start.1 = (bf16[16,4864]{1,0:T(8,128)(2,1)S(1)}, bf16[16,4864]{1,0:T(8,128)(2,1)S(1)}, u32[]{:S(2)}, u32[]{:S(2)}) collective-permute-start(bf16[16,4864]{1,0:T(8,128)(2,1)S(1)} %slice.278), channel_id=1, source_target_pairs={{0,28},{4,0},{8,4},{12,8},{16,12},{20,16},{24,20},{28,24},{1,29},{... | collective-permute-start | bytes 466952 | tf_op jit(solution)/shard_map/ppermute | solution.py:18
  8.2 1.3 collective-permute-start.4
  9.5 1.4 %collective-permute-start.5 = (bf16[16,8192]{1,0:T(8,128)(2,1)}, bf16[16,8192]{1,0:T(8,128)(2,1)S(1)}, u32[]{:S(2)}, u32[]{:S(2)}) collective-permute-start(bf16[16,8192]{1,0:T(8,128)(2,1)} %bitcast.48), channel_id=1, source_target_pairs={{0,3},{1,0},{2,1},{3,2},{4,7},{5,4},{6,5},{7,6},{8,11},{9,8},{10,9... | collective-permute-start | bytes 786440 | tf_op jit(solution)/shard_map/ppermute | solution.py:18
  10.9 1.7 %constant_dynamic-update-slice_fusion.10 = bf16[512,8192]{1,0:T(8,128)(2,1)} fusion(bf16[8192,16]{0,1:T(8,128)(2,1)} %param.5), kind=kLoop, calls=%fused_computation.71 | loop fusion | bytes 524288
  13.6 2.7 %collective-permute-start.3 = (bf16[16,4864]{1,0:T(8,128)(2,1)S(1)}, bf16[16,4864]{1,0:T(8,128)(2,1)S(1)}, u32[]{:S(2)}, u32[]{:S(2)}) collective-permute-start(bf16[16,4864]{1,0:T(8,128)(2,1)S(1)} %collective-permute-done.1), channel_id=1, source_target_pairs={{0,28},{4,0},{8,4},{12,8},{16,12},{20,16},{24,20},{28,24},{1,29},{... | collective-permute-start | bytes 466952 | tf_op jit(solution)/shard_map/ppermute | solution.py:18
  16.7 2.7 %collective-permute-start.9 = (bf16[16,4096]{1,0:T(8,128)(2,1)S(1)}, bf16[16,4096]{1,0:T(8,128)(2,1)S(1)}, u32[]{:S(2)}, u32[]{:S(2)}) collective-permute-start(bf16[16,4096]{1,0:T(8,128)(2,1)S(1)} %slice.281), channel_id=1, source_target_pairs={{0,3},{1,0},{2,1},{3,2},{4,7},{5,4},{6,5},{7,6},{8,11},{9,8},{10,9... | collective-permute-start | bytes 393224 | tf_op jit(solution)/shard_map/ppermute | solution.py:18
  19.5 2.7 %collective-permute-start.13 = (bf16[16,4864]{1,0:T(8,128)(2,1)S(1)}, bf16[16,4864]{1,0:T(8,128)(2,1)S(1)}, u32[]{:S(2)}, u32[]{:S(2)}) collective-permute-start(bf16[16,4864]{1,0:T(8,128)(2,1)S(1)} %collective-permute-done.3), channel_id=1, source_target_pairs={{0,28},{4,0},{8,4},{12,8},{16,12},{20,16},{24,20},{28,24},{1,29},{... | collective-permute-start | bytes 466952 | tf_op jit(solution)/shard_map/ppermute | solution.py:18
  22.3 2.7 %collective-permute-start.7 = (bf16[64,4864]{1,0:T(8,128)(2,1)S(1)}, bf16[64,4864]{1,0:T(8,128)(2,1)S(1)}, u32[]{:S(2)}, u32[]{:S(2)}) collective-permute-start(bf16[64,4864]{1,0:T(8,128)(2,1)S(1)} %constant_dynamic-update-slice_fusion), channel_id=1, source_target_pairs={{0,3},{1,0},{2,1},{3,2},{4,7},{5,4},{6,5},{7,6},{8,11},{9,8},{10,9... | collective-permute-start | bytes 1867784 | tf_op jit(solution)/shard_map/ppermute | solution.py:18
  25.1 2.7 %collective-permute-start.15 = (bf16[16,2432]{1,0:T(8,128)(2,1)S(1)}, bf16[16,2432]{1,0:T(8,128)(2,1)S(1)}, u32[]{:S(2)}, u32[]{:S(2)}) collective-permute-start(bf16[16,2432]{1,0:T(8,128)(2,1)S(1)} %slice.283), channel_id=1, source_target_pairs={{0,28},{4,0},{8,4},{12,8},{16,12},{20,16},{24,20},{28,24},{1,29},{... | collective-permute-start | bytes 233480 | tf_op jit(solution)/shard_map/ppermute | solution.py:18
  28.0 1.9 %collective-permute-done.14 = bf16[16,2432]{1,0:T(8,128)(2,1)S(1)} collective-permute-done((bf16[16,2432]{1,0:T(8,128)(2,1)S(1)}, bf16[16,2432]{1,0:T(8,128)(2,1)S(1)}, u32[]{:S(2)}, u32[]{:S(2)}) %collective-permute-start.14) | collective-permute-done | bytes 77856 | tf_op jit(solution)/shard_map/ppermute | solution.py:18
  30.7 7.4 %collective-permute-done.10 = bf16[64,3328]{1,0:T(8,128)(2,1)S(1)} collective-permute-done((bf16[64,3328]{1,0:T(8,128)(2,1)S(1)}, bf16[64,3328]{1,0:T(8,128)(2,1)S(1)}, u32[]{:S(2)}, u32[]{:S(2)}) %collective-permute-start.10) | collective-permute-done | bytes 426016 | tf_op jit(solution)/shard_map/ppermute | solution.py:18
  38.1 2.7 %collective-permute-start.17 = (bf16[64,3328]{1,0:T(8,128)(2,1)S(1)}, bf16[64,3328]{1,0:T(8,128)(2,1)S(1)}, u32[]{:S(2)}, u32[]{:S(2)}) collective-permute-start(bf16[64,3328]{1,0:T(8,128)(2,1)S(1)} %collective-permute-done.11), channel_id=1, source_target_pairs={{0,28},{4,0},{8,4},{12,8},{16,12},{20,16},{24,20},{28,24},{1,29},{... | collective-permute-start | bytes 1277960 | tf_op jit(solution)/shard_map/ppermute | solution.py:18
  40.8 1.5 %collective-permute-start.24 = (bf16[48,4864]{1,0:T(8,128)(2,1)S(1)}, bf16[48,4864]{1,0:T(8,128)(2,1)S(1)}, u32[]{:S(2)}, u32[]{:S(2)}) collective-permute-start(bf16[48,4864]{1,0:T(8,128)(2,1)S(1)} %maximum_maximum_fusion), channel_id=1, source_target_pairs={{0,3},{1,0},{2,1},{3,2},{4,7},{5,4},{6,5},{7,6},{8,11},{9,8},{10,9... | collective-permute-start | bytes 1400840 | tf_op jit(solution)/shard_map/ppermute | solution.py:18
  43.3 3.0 %collective-permute-done.16 = bf16[64,3328]{1,0:T(8,128)(2,1)S(1)} collective-permute-done((bf16[64,3328]{1,0:T(8,128)(2,1)S(1)}, bf16[64,3328]{1,0:T(8,128)(2,1)S(1)}, u32[]{:S(2)}, u32[]{:S(2)}) %collective-permute-start.16) | collective-permute-done | bytes 426016 | tf_op jit(solution)/shard_map/ppermute | solution.py:18
  46.2 1.7 %collective-permute-start.21 = (bf16[64,2432]{1,0:T(8,128)(2,1)S(1)}, bf16[64,2432]{1,0:T(8,128)(2,1)S(1)}, u32[]{:S(2)}, u32[]{:S(2)}) collective-permute-start(bf16[64,2432]{1,0:T(8,128)(2,1)S(1)} %slice.222), channel_id=1, source_target_pairs={{0,3},{1,0},{2,1},{3,2},{4,7},{5,4},{6,5},{7,6},{8,11},{9,8},{10,9... | collective-permute-start | bytes 933896 | tf_op jit(solution)/shard_map/ppermute | solution.py:18
  48.9 8.2 %collective-permute-done.20 = bf16[64,2432]{1,0:T(8,128)(2,1)S(1)} collective-permute-done((bf16[64,2432]{1,0:T(8,128)(2,1)S(1)}, bf16[64,2432]{1,0:T(8,128)(2,1)S(1)}, u32[]{:S(2)}, u32[]{:S(2)}) %collective-permute-start.20) | collective-permute-done | bytes 311328 | tf_op jit(solution)/shard_map/ppermute | solution.py:18
  57.6 2.7 %collective-permute-start.27 = (bf16[48,2432]{1,0:T(8,128)(2,1)S(1)}, bf16[48,2432]{1,0:T(8,128)(2,1)S(1)}, u32[]{:S(2)}, u32[]{:S(2)}) collective-permute-start(bf16[48,2432]{1,0:T(8,128)(2,1)S(1)} %slice.290), channel_id=1, source_target_pairs={{0,3},{1,0},{2,1},{3,2},{4,7},{5,4},{6,5},{7,6},{8,11},{9,8},{10,9... | collective-permute-start | bytes 700424 | tf_op jit(solution)/shard_map/ppermute | solution.py:18
  60.4 4.7 %collective-permute-done.26 = bf16[48,2432]{1,0:T(8,128)(2,1)S(1)} collective-permute-done((bf16[48,2432]{1,0:T(8,128)(2,1)S(1)}, bf16[48,2432]{1,0:T(8,128)(2,1)S(1)}, u32[]{:S(2)}, u32[]{:S(2)}) %collective-permute-start.26) | collective-permute-done | bytes 233504 | tf_op jit(solution)/shard_map/ppermute | solution.py:18
  65.4 2.7 %collective-permute-start.23 = (bf16[64,1664]{1,0:T(8,128)(2,1)S(1)}, bf16[64,1664]{1,0:T(8,128)(2,1)S(1)}, u32[]{:S(2)}, u32[]{:S(2)}) collective-permute-start(bf16[64,1664]{1,0:T(8,128)(2,1)S(1)} %slice.226), channel_id=1, source_target_pairs={{0,28},{4,0},{8,4},{12,8},{16,12},{20,16},{24,20},{28,24},{1,29},{... | collective-permute-start | bytes 638984 | tf_op jit(solution)/shard_map/ppermute | solution.py:18
  68.1 3.4 %collective-permute-done.22 = bf16[64,1664]{1,0:T(8,128)(2,1)S(1)} collective-permute-done((bf16[64,1664]{1,0:T(8,128)(2,1)S(1)}, bf16[64,1664]{1,0:T(8,128)(2,1)S(1)}, u32[]{:S(2)}, u32[]{:S(2)}) %collective-permute-start.22) | collective-permute-done | bytes 213024 | tf_op jit(solution)/shard_map/ppermute | solution.py:18
  71.6 1.3 collective-permute-done.23
  73.8 2.3 %fusion.27 = f32[512,256]{1,0:T(8,128)S(1)} fusion(bf16[512,8192]{1,0:T(8,128)(2,1)S(1)} %maximum_dynamic-update-slice_fusion, bf16[8192,256]{1,0:T(8,128)(2,1)S(1)} %copy-done.4), kind=kOutput, calls=%fused_computation.92 | convolution fusion | flops 2147483648 | bytes 13107200 | tf_op jit(solution)/shard_map/dot_general | solution.py:93
  77.1 9.4 %collective-permute-start.28 = (f32[2,8,16,256]{3,2,1,0:T(8,128)S(1)}, f32[2,8,16,256]{3,2,1,0:T(8,128)S(1)}, u32[]{:S(2)}, u32[]{:S(2)}) collective-permute-start(f32[2,8,16,256]{3,2,1,0:T(8,128)S(1)} %fusion.8), channel_id=1, source_target_pairs={{0,32},{32,0},{1,33},{33,1},{2,34},{34,2},{3,35},{35,3},{4,36},{36... | collective-permute-start | bytes 786440 | tf_op jit(solution)/shard_map/ppermute | solution.py:18
  86.5 1.2 collective-permute-done.28
  88.9 11.5 %all-to-all-start = ((bf16[128,4,128]{2,1,0:T(4,128)(2,1)}), bf16[128,4,128]{2,1,0:T(4,128)(2,1)S(1)}, u32[]{:S(2)}, u32[]{:S(2)}) async-start(bf16[128,4,128]{2,1,0:T(4,128)(2,1)} %copy.15), calls=%async_computation | async-start | bytes 262144 | tf_op jit(solution)/shard_map/all_to_all | solution.py:102
  100.6 10.7 %all-to-all-done = bf16[128,4,128]{2,1,0:T(4,128)(2,1)S(1)} async-done(((bf16[128,4,128]{2,1,0:T(4,128)(2,1)}), bf16[128,4,128]{2,1,0:T(4,128)(2,1)S(1)}, u32[]{:S(2)}, u32[]{:S(2)}) %all-to-all-start) | async-done | bytes 131104 | tf_op jit(solution)/shard_map/all_to_all | solution.py:102
  112.0 17.0 %all_to_all.10 = bf16[128,4,128]{2,1,0:T(4,128)(2,1)S(1)} all-to-all(bf16[128,4,128]{2,1,0:T(4,128)(2,1)S(1)} %bitcast.51), channel_id=1, replica_groups=mesh['x'=4,'core'=2,'z'=8,'y'=4] {'x','z','y'}, dimensions={0} | all-to-all | bytes 262144 | tf_op jit(solution)/shard_map/all_to_all | solution.py:114
  129.1 3.1 %collective-permute-start.29 = (bf16[256,256]{0,1:T(8,128)(2,1)S(1)}, bf16[256,256]{0,1:T(8,128)(2,1)S(1)}, u32[]{:S(2)}, u32[]{:S(2)}) collective-permute-start(bf16[256,256]{0,1:T(8,128)(2,1)S(1)} %bitcast.56), channel_id=1, source_target_pairs={{0,32},{32,0},{1,33},{33,1},{2,34},{34,2},{3,35},{35,3},{4,36},{36... | collective-permute-start | bytes 393224 | tf_op jit(solution)/shard_map/ppermute | solution.py:18
  132.2 1.0 collective-permute-done.29
  133.6 7.8 %convolution_convert_fusion = bf16[8192,256]{1,0:T(8,128)(2,1)} fusion(bf16[512,8192]{1,0:T(8,128)(2,1)} %copy-done.2, bf16[512,256]{1,0:T(8,128)(2,1)S(1)} %bitcast.58), kind=kOutput, calls=%fused_computation | convolution fusion | flops 2149580800 | bytes 12845056 | tf_op jit(solution)/shard_map/dot_general | solution.py:122
  (136 shorter events, 10.1 us)
Async XLA Ops:
  0.6 110.7 %copy-start = (f32[128,128]{1,0:T(8,128)S(1)}, f32[128,128]{1,0:T(8,128)}, u32[]{:S(2)}) copy-start(f32[128,128]{1,0:T(8,128)} %param.9) | copy-start | bytes 196612
  1.6 11.9 %collective-permute-start = (bf16[16,4864]{1,0:T(8,128)(2,1)S(1)}, bf16[16,4864]{1,0:T(8,128)(2,1)S(1)}, u32[]{:S(2)}, u32[]{:S(2)}) collective-permute-start(bf16[16,4864]{1,0:T(8,128)(2,1)S(1)} %slice.278), channel_id=1, source_target_pairs={{0,4},{4,8},{8,12},{12,16},{16,20},{20,24},{24,28},{28,0},{1,5},{5... | collective-permute-start | bytes 466952 | tf_op jit(solution)/shard_map/ppermute | solution.py:18
  4.1 9.5 %collective-permute-start.1 = (bf16[16,4864]{1,0:T(8,128)(2,1)S(1)}, bf16[16,4864]{1,0:T(8,128)(2,1)S(1)}, u32[]{:S(2)}, u32[]{:S(2)}) collective-permute-start(bf16[16,4864]{1,0:T(8,128)(2,1)S(1)} %slice.278), channel_id=1, source_target_pairs={{0,28},{4,0},{8,4},{12,8},{16,12},{20,16},{24,20},{28,24},{1,29},{... | collective-permute-start | bytes 466952 | tf_op jit(solution)/shard_map/ppermute | solution.py:18
  8.2 8.4 %collective-permute-start.4 = (bf16[16,8192]{1,0:T(8,128)(2,1)}, bf16[16,8192]{1,0:T(8,128)(2,1)S(1)}, u32[]{:S(2)}, u32[]{:S(2)}) collective-permute-start(bf16[16,8192]{1,0:T(8,128)(2,1)} %bitcast.47), channel_id=1, source_target_pairs={{0,1},{1,2},{2,3},{3,0},{4,5},{5,6},{6,7},{7,4},{8,9},{9,10},{10,1... | collective-permute-start | bytes 786440 | tf_op jit(solution)/shard_map/ppermute | solution.py:18
  9.5 7.2 %collective-permute-start.5 = (bf16[16,8192]{1,0:T(8,128)(2,1)}, bf16[16,8192]{1,0:T(8,128)(2,1)S(1)}, u32[]{:S(2)}, u32[]{:S(2)}) collective-permute-start(bf16[16,8192]{1,0:T(8,128)(2,1)} %bitcast.48), channel_id=1, source_target_pairs={{0,3},{1,0},{2,1},{3,2},{4,7},{5,4},{6,5},{7,6},{8,11},{9,8},{10,9... | collective-permute-start | bytes 786440 | tf_op jit(solution)/shard_map/ppermute | solution.py:18
  13.5 5.9 %collective-permute-start.2 = (bf16[16,4864]{1,0:T(8,128)(2,1)S(1)}, bf16[16,4864]{1,0:T(8,128)(2,1)S(1)}, u32[]{:S(2)}, u32[]{:S(2)}) collective-permute-start(bf16[16,4864]{1,0:T(8,128)(2,1)S(1)} %collective-permute-done), channel_id=1, source_target_pairs={{0,4},{4,8},{8,12},{12,16},{16,20},{20,24},{24,28},{28,0},{1,5},{5... | collective-permute-start | bytes 466952 | tf_op jit(solution)/shard_map/ppermute | solution.py:18
  13.6 5.8 %collective-permute-start.3 = (bf16[16,4864]{1,0:T(8,128)(2,1)S(1)}, bf16[16,4864]{1,0:T(8,128)(2,1)S(1)}, u32[]{:S(2)}, u32[]{:S(2)}) collective-permute-start(bf16[16,4864]{1,0:T(8,128)(2,1)S(1)} %collective-permute-done.1), channel_id=1, source_target_pairs={{0,28},{4,0},{8,4},{12,8},{16,12},{20,16},{24,20},{28,24},{1,29},{... | collective-permute-start | bytes 466952 | tf_op jit(solution)/shard_map/ppermute | solution.py:18
  16.6 5.7 %collective-permute-start.8 = (bf16[16,4096]{1,0:T(8,128)(2,1)S(1)}, bf16[16,4096]{1,0:T(8,128)(2,1)S(1)}, u32[]{:S(2)}, u32[]{:S(2)}) collective-permute-start(bf16[16,4096]{1,0:T(8,128)(2,1)S(1)} %slice.280), channel_id=1, source_target_pairs={{0,1},{1,2},{2,3},{3,0},{4,5},{5,6},{6,7},{7,4},{8,9},{9,10},{10,1... | collective-permute-start | bytes 393224 | tf_op jit(solution)/shard_map/ppermute | solution.py:18
  16.7 8.2 %collective-permute-start.9 = (bf16[16,4096]{1,0:T(8,128)(2,1)S(1)}, bf16[16,4096]{1,0:T(8,128)(2,1)S(1)}, u32[]{:S(2)}, u32[]{:S(2)}) collective-permute-start(bf16[16,4096]{1,0:T(8,128)(2,1)S(1)} %slice.281), channel_id=1, source_target_pairs={{0,3},{1,0},{2,1},{3,2},{4,7},{5,4},{6,5},{7,6},{8,11},{9,8},{10,9... | collective-permute-start | bytes 393224 | tf_op jit(solution)/shard_map/ppermute | solution.py:18
  19.5 5.5 %collective-permute-start.12 = (bf16[16,4864]{1,0:T(8,128)(2,1)S(1)}, bf16[16,4864]{1,0:T(8,128)(2,1)S(1)}, u32[]{:S(2)}, u32[]{:S(2)}) collective-permute-start(bf16[16,4864]{1,0:T(8,128)(2,1)S(1)} %collective-permute-done.2), channel_id=1, source_target_pairs={{0,4},{4,8},{8,12},{12,16},{16,20},{20,24},{24,28},{28,0},{1,5},{5... | collective-permute-start | bytes 466952 | tf_op jit(solution)/shard_map/ppermute | solution.py:18
  19.5 5.6 %collective-permute-start.13 = (bf16[16,4864]{1,0:T(8,128)(2,1)S(1)}, bf16[16,4864]{1,0:T(8,128)(2,1)S(1)}, u32[]{:S(2)}, u32[]{:S(2)}) collective-permute-start(bf16[16,4864]{1,0:T(8,128)(2,1)S(1)} %collective-permute-done.3), channel_id=1, source_target_pairs={{0,28},{4,0},{8,4},{12,8},{16,12},{20,16},{24,20},{28,24},{1,29},{... | collective-permute-start | bytes 466952 | tf_op jit(solution)/shard_map/ppermute | solution.py:18
  22.2 18.5 %collective-permute-start.6 = (bf16[64,4864]{1,0:T(8,128)(2,1)S(1)}, bf16[64,4864]{1,0:T(8,128)(2,1)S(1)}, u32[]{:S(2)}, u32[]{:S(2)}) collective-permute-start(bf16[64,4864]{1,0:T(8,128)(2,1)S(1)} %constant_dynamic-update-slice_fusion), channel_id=1, source_target_pairs={{0,1},{1,2},{2,3},{3,0},{4,5},{5,6},{6,7},{7,4},{8,9},{9,10},{10,1... | collective-permute-start | bytes 1867784 | tf_op jit(solution)/shard_map/ppermute | solution.py:18
  22.3 18.4 %collective-permute-start.7 = (bf16[64,4864]{1,0:T(8,128)(2,1)S(1)}, bf16[64,4864]{1,0:T(8,128)(2,1)S(1)}, u32[]{:S(2)}, u32[]{:S(2)}) collective-permute-start(bf16[64,4864]{1,0:T(8,128)(2,1)S(1)} %constant_dynamic-update-slice_fusion), channel_id=1, source_target_pairs={{0,3},{1,0},{2,1},{3,2},{4,7},{5,4},{6,5},{7,6},{8,11},{9,8},{10,9... | collective-permute-start | bytes 1867784 | tf_op jit(solution)/shard_map/ppermute | solution.py:18
  25.0 4.8 %collective-permute-start.14 = (bf16[16,2432]{1,0:T(8,128)(2,1)S(1)}, bf16[16,2432]{1,0:T(8,128)(2,1)S(1)}, u32[]{:S(2)}, u32[]{:S(2)}) collective-permute-start(bf16[16,2432]{1,0:T(8,128)(2,1)S(1)} %slice.282), channel_id=1, source_target_pairs={{0,4},{4,8},{8,12},{12,16},{16,20},{20,24},{24,28},{28,0},{1,5},{5... | collective-permute-start | bytes 233480 | tf_op jit(solution)/shard_map/ppermute | solution.py:18
  25.1 5.5 %collective-permute-start.15 = (bf16[16,2432]{1,0:T(8,128)(2,1)S(1)}, bf16[16,2432]{1,0:T(8,128)(2,1)S(1)}, u32[]{:S(2)}, u32[]{:S(2)}) collective-permute-start(bf16[16,2432]{1,0:T(8,128)(2,1)S(1)} %slice.283), channel_id=1, source_target_pairs={{0,28},{4,0},{8,4},{12,8},{16,12},{20,16},{24,20},{28,24},{1,29},{... | collective-permute-start | bytes 233480 | tf_op jit(solution)/shard_map/ppermute | solution.py:18
  27.9 10.2 %collective-permute-start.10 = (bf16[64,3328]{1,0:T(8,128)(2,1)S(1)}, bf16[64,3328]{1,0:T(8,128)(2,1)S(1)}, u32[]{:S(2)}, u32[]{:S(2)}) collective-permute-start(bf16[64,3328]{1,0:T(8,128)(2,1)S(1)} %pad_maximum_fusion.1), channel_id=1, source_target_pairs={{0,4},{4,8},{8,12},{12,16},{16,20},{20,24},{24,28},{28,0},{1,5},{5... | collective-permute-start | bytes 1277960 | tf_op jit(solution)/shard_map/ppermute | solution.py:18
  29.8 8.2 %collective-permute-start.11 = (bf16[64,3328]{1,0:T(8,128)(2,1)S(1)}, bf16[64,3328]{1,0:T(8,128)(2,1)S(1)}, u32[]{:S(2)}, u32[]{:S(2)}) collective-permute-start(bf16[64,3328]{1,0:T(8,128)(2,1)S(1)} %pad_maximum_fusion.1), channel_id=1, source_target_pairs={{0,28},{4,0},{8,4},{12,8},{16,12},{20,16},{24,20},{28,24},{1,29},{... | collective-permute-start | bytes 1277960 | tf_op jit(solution)/shard_map/ppermute | solution.py:18
  38.1 8.2 %collective-permute-start.16 = (bf16[64,3328]{1,0:T(8,128)(2,1)S(1)}, bf16[64,3328]{1,0:T(8,128)(2,1)S(1)}, u32[]{:S(2)}, u32[]{:S(2)}) collective-permute-start(bf16[64,3328]{1,0:T(8,128)(2,1)S(1)} %collective-permute-done.10), channel_id=1, source_target_pairs={{0,4},{4,8},{8,12},{12,16},{16,20},{20,24},{24,28},{28,0},{1,5},{5... | collective-permute-start | bytes 1277960 | tf_op jit(solution)/shard_map/ppermute | solution.py:18
  38.1 9.9 %collective-permute-start.17 = (bf16[64,3328]{1,0:T(8,128)(2,1)S(1)}, bf16[64,3328]{1,0:T(8,128)(2,1)S(1)}, u32[]{:S(2)}, u32[]{:S(2)}) collective-permute-start(bf16[64,3328]{1,0:T(8,128)(2,1)S(1)} %collective-permute-done.11), channel_id=1, source_target_pairs={{0,28},{4,0},{8,4},{12,8},{16,12},{20,16},{24,20},{28,24},{1,29},{... | collective-permute-start | bytes 1277960 | tf_op jit(solution)/shard_map/ppermute | solution.py:18
  40.8 16.7 %collective-permute-start.24 = (bf16[48,4864]{1,0:T(8,128)(2,1)S(1)}, bf16[48,4864]{1,0:T(8,128)(2,1)S(1)}, u32[]{:S(2)}, u32[]{:S(2)}) collective-permute-start(bf16[48,4864]{1,0:T(8,128)(2,1)S(1)} %maximum_maximum_fusion), channel_id=1, source_target_pairs={{0,3},{1,0},{2,1},{3,2},{4,7},{5,4},{6,5},{7,6},{8,11},{9,8},{10,9... | collective-permute-start | bytes 1400840 | tf_op jit(solution)/shard_map/ppermute | solution.py:18
  42.2 15.2 %collective-permute-start.25 = (bf16[48,4864]{1,0:T(8,128)(2,1)S(1)}, bf16[48,4864]{1,0:T(8,128)(2,1)S(1)}, u32[]{:S(2)}, u32[]{:S(2)}) collective-permute-start(bf16[48,4864]{1,0:T(8,128)(2,1)S(1)} %maximum_maximum_fusion), channel_id=1, source_target_pairs={{0,1},{1,2},{2,3},{3,0},{4,5},{5,6},{6,7},{7,4},{8,9},{9,10},{10,1... | collective-permute-start | bytes 1400840 | tf_op jit(solution)/shard_map/ppermute | solution.py:18
  42.3 14.7 %collective-permute-start.20 = (bf16[64,2432]{1,0:T(8,128)(2,1)S(1)}, bf16[64,2432]{1,0:T(8,128)(2,1)S(1)}, u32[]{:S(2)}, u32[]{:S(2)}) collective-permute-start(bf16[64,2432]{1,0:T(8,128)(2,1)S(1)} %slice.221), channel_id=1, source_target_pairs={{0,1},{1,2},{2,3},{3,0},{4,5},{5,6},{6,7},{7,4},{8,9},{9,10},{10,1... | collective-permute-start | bytes 933896 | tf_op jit(solution)/shard_map/ppermute | solution.py:18
  46.2 11.1 %collective-permute-start.21 = (bf16[64,2432]{1,0:T(8,128)(2,1)S(1)}, bf16[64,2432]{1,0:T(8,128)(2,1)S(1)}, u32[]{:S(2)}, u32[]{:S(2)}) collective-permute-start(bf16[64,2432]{1,0:T(8,128)(2,1)S(1)} %slice.222), channel_id=1, source_target_pairs={{0,3},{1,0},{2,1},{3,2},{4,7},{5,4},{6,5},{7,6},{8,11},{9,8},{10,9... | collective-permute-start | bytes 933896 | tf_op jit(solution)/shard_map/ppermute | solution.py:18
  48.0 17.2 %collective-permute-start.18 = (bf16[64,3328]{1,0:T(8,128)(2,1)S(1)}, bf16[64,3328]{1,0:T(8,128)(2,1)S(1)}, u32[]{:S(2)}, u32[]{:S(2)}) collective-permute-start(bf16[64,3328]{1,0:T(8,128)(2,1)S(1)} %collective-permute-done.16), channel_id=1, source_target_pairs={{0,4},{4,8},{8,12},{12,16},{16,20},{20,24},{24,28},{28,0},{1,5},{5... | collective-permute-start | bytes 1277960 | tf_op jit(solution)/shard_map/ppermute | solution.py:18
  57.0 8.1 %collective-permute-start.19 = (bf16[64,3328]{1,0:T(8,128)(2,1)S(1)}, bf16[64,3328]{1,0:T(8,128)(2,1)S(1)}, u32[]{:S(2)}, u32[]{:S(2)}) collective-permute-start(bf16[64,3328]{1,0:T(8,128)(2,1)S(1)} %collective-permute-done.17), channel_id=1, source_target_pairs={{0,28},{4,0},{8,4},{12,8},{16,12},{20,16},{24,20},{28,24},{1,29},{... | collective-permute-start | bytes 1277960 | tf_op jit(solution)/shard_map/ppermute | solution.py:18
  57.4 7.6 %collective-permute-start.26 = (bf16[48,2432]{1,0:T(8,128)(2,1)S(1)}, bf16[48,2432]{1,0:T(8,128)(2,1)S(1)}, u32[]{:S(2)}, u32[]{:S(2)}) collective-permute-start(bf16[48,2432]{1,0:T(8,128)(2,1)S(1)} %slice.289), channel_id=1, source_target_pairs={{0,1},{1,2},{2,3},{3,0},{4,5},{5,6},{6,7},{7,4},{8,9},{9,10},{10,1... | collective-permute-start | bytes 700424 | tf_op jit(solution)/shard_map/ppermute | solution.py:18
  57.6 7.5 %collective-permute-start.27 = (bf16[48,2432]{1,0:T(8,128)(2,1)S(1)}, bf16[48,2432]{1,0:T(8,128)(2,1)S(1)}, u32[]{:S(2)}, u32[]{:S(2)}) collective-permute-start(bf16[48,2432]{1,0:T(8,128)(2,1)S(1)} %slice.290), channel_id=1, source_target_pairs={{0,3},{1,0},{2,1},{3,2},{4,7},{5,4},{6,5},{7,6},{8,11},{9,8},{10,9... | collective-permute-start | bytes 700424 | tf_op jit(solution)/shard_map/ppermute | solution.py:18
  65.3 6.3 %collective-permute-start.22 = (bf16[64,1664]{1,0:T(8,128)(2,1)S(1)}, bf16[64,1664]{1,0:T(8,128)(2,1)S(1)}, u32[]{:S(2)}, u32[]{:S(2)}) collective-permute-start(bf16[64,1664]{1,0:T(8,128)(2,1)S(1)} %slice.225), channel_id=1, source_target_pairs={{0,4},{4,8},{8,12},{12,16},{16,20},{20,24},{24,28},{28,0},{1,5},{5... | collective-permute-start | bytes 638984 | tf_op jit(solution)/shard_map/ppermute | solution.py:18
  65.4 7.5 %collective-permute-start.23 = (bf16[64,1664]{1,0:T(8,128)(2,1)S(1)}, bf16[64,1664]{1,0:T(8,128)(2,1)S(1)}, u32[]{:S(2)}, u32[]{:S(2)}) collective-permute-start(bf16[64,1664]{1,0:T(8,128)(2,1)S(1)} %slice.226), channel_id=1, source_target_pairs={{0,28},{4,0},{8,4},{12,8},{16,12},{20,16},{24,20},{28,24},{1,29},{... | collective-permute-start | bytes 638984 | tf_op jit(solution)/shard_map/ppermute | solution.py:18
  77.1 10.6 %collective-permute-start.28 = (f32[2,8,16,256]{3,2,1,0:T(8,128)S(1)}, f32[2,8,16,256]{3,2,1,0:T(8,128)S(1)}, u32[]{:S(2)}, u32[]{:S(2)}) collective-permute-start(f32[2,8,16,256]{3,2,1,0:T(8,128)S(1)} %fusion.8), channel_id=1, source_target_pairs={{0,32},{32,0},{1,33},{33,1},{2,34},{34,2},{3,35},{35,3},{4,36},{36... | collective-permute-start | bytes 786440 | tf_op jit(solution)/shard_map/ppermute | solution.py:18
  88.9 22.4 %all-to-all-start = ((bf16[128,4,128]{2,1,0:T(4,128)(2,1)}), bf16[128,4,128]{2,1,0:T(4,128)(2,1)S(1)}, u32[]{:S(2)}, u32[]{:S(2)}) async-start(bf16[128,4,128]{2,1,0:T(4,128)(2,1)} %copy.15), calls=%async_computation | async-start | bytes 262144 | tf_op jit(solution)/shard_map/all_to_all | solution.py:102
  129.1 4.1 %collective-permute-start.29 = (bf16[256,256]{0,1:T(8,128)(2,1)S(1)}, bf16[256,256]{0,1:T(8,128)(2,1)S(1)}, u32[]{:S(2)}, u32[]{:S(2)}) collective-permute-start(bf16[256,256]{0,1:T(8,128)(2,1)S(1)} %bitcast.56), channel_id=1, source_target_pairs={{0,32},{32,0},{1,33},{33,1},{2,34},{34,2},{3,35},{35,3},{4,36},{36... | collective-permute-start | bytes 393224 | tf_op jit(solution)/shard_map/ppermute | solution.py:18
  (5 other events, 92.3 us)
